TPU v7x, 256 devices: a whole 4x4x8 slice. The times are simulated.
256 devices in a mesh: expert: 16 (over y_lo, x, core), dp: 16 (over y_hi, z).
Axes of the slice: x: 4, y: 4 (y_hi: 2, y_lo: 2; y = y_hi * 2 + y_lo), z: 8, core: 2. Of those that a mesh axis runs over, the one named last changes fastest.
Arguments:
- attn_input: bfloat16 [12288, 4096], P('dp'), may hold values from -6 to 6
- query_grad: bfloat16 [12288, 8192], P('dp', 'expert'), may hold values from -6 to 6
- query_weight: float32 [8192, 4096], P(('expert', 'dp')), may hold values from -40 to 40
- moe_cotangent: bfloat16 [2048, 4096], P('expert', 'dp'), may hold values from -6 to 6
- expert_ids: int32 [2048, 8], P('expert'), may hold values from 0 to 31, all different within a row; in each aligned block of 128 rows (0 to 127, 128 to 255, ...) at most 40 rows name the same one
- route_weights: float32 [2048, 8], P('expert'), may hold values from 0.2 to 1
- gate_saved: bfloat16 [640, 32, 1536], P('dp', 'expert'), may hold values from -6 to 6
- up_saved: bfloat16 [640, 32, 1536], P('dp', 'expert'), may hold values from -6 to 6
- gate_weight: bfloat16 [32, 4096, 1536], P('expert', 'dp'), may hold values from -0.09375 to 0.09375
- up_weight: bfloat16 [32, 4096, 1536], P('expert', 'dp'), may hold values from -0.09375 to 0.09375
- down_weight: bfloat16 [32, 1536, 4096], P('expert', None, 'dp'), may hold values from -0.15625 to 0.15625
Outputs:
- query_weight_next: float32 [8192, 4096], P(('expert', 'dp'))
- moe_input_grad: float32 [2048, 4096], P('expert', 'dp')
Inputs may be any that keep to these rules, and one draw needn't show every extreme that they name: `expert_ids`: in each aligned block of 128 rows no expert is named by more than 40 rows, and one expert by exactly 40 rows in some block; each row names 8 different experts.
All inputs are finite; a program needn't handle non-finite values.
Results may differ from a plain program's by a relative error of at most 0.022.
Values may be sent and summed in bfloat16 or wider, within the bound.
A program may use at most 128 MiB of HBM per device.

v0:
```python
import jax
import jax.numpy as jnp
from jax import lax
from jax.sharding import PartitionSpec as P

step_rate = 0.01
epsilon = 1e-06


def slot_tables(expert_ids, route_weights, experts, capacity):
    expert_iota = lax.broadcasted_iota(jnp.int32, (1, 1, experts), 2)
    chosen = (expert_ids[:, :, None] == expert_iota).astype(jnp.int32)
    counts = jnp.sum(chosen, axis=1, dtype=jnp.int32)
    before = jnp.cumsum(counts, axis=0, dtype=jnp.int32) - counts
    position = jnp.sum(chosen * before[:, None, :], axis=2, dtype=jnp.int32)
    slot_code = position * experts + expert_ids
    slot_iota = lax.broadcasted_iota(jnp.int32, (1, 1, capacity * experts), 2)
    matched = slot_code[:, :, None] == slot_iota
    select = jnp.sum(matched.astype(jnp.float32), axis=1)
    scaled = jnp.sum(jnp.where(matched, route_weights[:, :, None], 0.0), axis=1)
    return (select, scaled)


def activation_grads(hidden, gate_vals, up_vals):
    gate_float = gate_vals.astype(jnp.float32)
    up_float = up_vals.astype(jnp.float32)
    sigmoid_vals = jax.nn.sigmoid(gate_float)
    gate_grad = hidden * up_float * sigmoid_vals * (1.0 + gate_float * (1.0 - sigmoid_vals))
    up_grad = hidden * gate_float * sigmoid_vals
    return jnp.stack([gate_grad, up_grad], axis=2).astype(jnp.bfloat16)


def weight_update(attn_input, query_grad, query_weight):
    gradient = lax.psum_scatter(
        lax.dot_general(
            query_grad, attn_input, (((0,), (0,)), ((), ())), preferred_element_type=jnp.float32
        ).astype(jnp.bfloat16),
        "dp",
        scatter_dimension=0,
        tiled=True,
    ).astype(jnp.float32)
    radial = jnp.mean(query_weight * gradient, axis=1, keepdims=True) / (
        jnp.mean(query_weight * query_weight, axis=1, keepdims=True) + epsilon
    )
    stepped = query_weight - step_rate * (gradient - radial * query_weight)
    return stepped * lax.rsqrt(jnp.mean(stepped * stepped, axis=1, keepdims=True) + epsilon)


def expert_update(
    moe_cotangent,
    expert_ids,
    route_weights,
    gate_saved,
    up_saved,
    gate_weight,
    up_weight,
    down_weight,
):
    groups = lax.axis_size("expert")
    experts = gate_weight.shape[0] * groups
    capacity = gate_saved.shape[0] * lax.axis_size("dp") // groups
    select, scaled = slot_tables(expert_ids, route_weights, experts, capacity)
    outgoing = jnp.dot(
        scaled.T,
        moe_cotangent.astype(jnp.float32),
        precision=lax.Precision.HIGHEST,
        preferred_element_type=jnp.float32,
    )
    outgoing = outgoing.astype(jnp.bfloat16).reshape(capacity, experts, moe_cotangent.shape[1])
    arrived = lax.all_to_all(outgoing, "expert", split_axis=1, concat_axis=0, tiled=True)
    hidden = lax.psum_scatter(
        jnp.einsum("sec,ehc->seh", arrived, down_weight, preferred_element_type=jnp.float32).astype(
            jnp.bfloat16
        ),
        "dp",
        scatter_dimension=0,
        tiled=True,
    ).astype(jnp.float32)
    grads_pair = activation_grads(hidden, gate_saved, up_saved)
    part_rows = lax.all_gather(grads_pair, "dp", axis=0, tiled=True)
    total = jnp.einsum(
        "seh,ech->sec", part_rows[:, :, 0], gate_weight, preferred_element_type=jnp.float32
    )
    total = total + jnp.einsum(
        "seh,ech->sec", part_rows[:, :, 1], up_weight, preferred_element_type=jnp.float32
    )
    slot_input = total.astype(jnp.bfloat16)
    returned_rows = lax.all_to_all(slot_input, "expert", split_axis=0, concat_axis=1, tiled=True)
    flat_rows = returned_rows.reshape(capacity * experts, returned_rows.shape[2])
    return jnp.dot(select.astype(jnp.bfloat16), flat_rows, preferred_element_type=jnp.float32)


def shards(
    attn_input,
    query_grad,
    query_weight,
    moe_cotangent,
    expert_ids,
    route_weights,
    gate_saved,
    up_saved,
    gate_weight,
    up_weight,
    down_weight,
):
    moe_input_grad = expert_update(
        moe_cotangent,
        expert_ids,
        route_weights,
        gate_saved,
        up_saved,
        gate_weight,
        up_weight,
        down_weight,
    )
    query_weight_next = weight_update(attn_input, query_grad, query_weight)
    return (query_weight_next, moe_input_grad)


def solution(mesh):
    placed = (
        P("dp", None),
        P("dp", "expert"),
        P(("expert", "dp"), None),
        P("expert", "dp"),
        P("expert", None),
        P("expert", None),
        P("dp", "expert", None),
        P("dp", "expert", None),
        P("expert", "dp", None),
        P("expert", "dp", None),
        P("expert", None, "dp"),
    )
    return jax.shard_map(
        shards,
        mesh=mesh,
        in_specs=placed,
        out_specs=(P(("expert", "dp"), None), P("expert", "dp")),
        check_vma=False,
    )
```

profile of v0, /device:TPU:1, one launch (start us, length us, event | category | flops | bytes accessed | tf_op | source)
XLA Modules:
  0.0 630.5 jit_solution(17766402492939068034)
XLA Ops:
  7.2 0.8 convert_reduce_fusion.1
  8.0 0.1 copy.35
  8.1 0.2 reduce_window_sum.11
  8.4 0.7 select_reduce_fusion.1
  9.1 0.7 multiply_add_fusion
  9.8 0.1 copy.38
  9.9 0.8 copy.39
  10.7 4.1 convert_reduce_fusion
  14.8 1.6 convolution_convert_fusion.2
  16.4 0.4 copy.40
  16.8 18.3 %all_to_all.33 = bf16[40,32,256]{2,0,1:T(8,128)(2,1)S(1)} all-to-all(bf16[40,32,256]{2,0,1:T(8,128)(2,1)S(1)} %copy.40), channel_id=1, replica_groups=mesh['expert'=16,'dp'=16] {'expert'}, dimensions={1} | all-to-all | bytes 1310720 | tf_op jit(solution)/shard_map/all_to_all | solution.py:70
  35.2 1.2 fusion.2
  36.4 2.5 copy.49
  38.9 1.1 copy-done.6
  40.0 7.8 %convolution_convert_fusion = bf16[512,4096]{1,0:T(8,128)(2,1)} fusion(bf16[768,512]{1,0:T(8,128)(2,1)S(1)} %copy-done.6, bf16[768,4096]{1,0:T(8,128)(2,1)} %param.11), kind=kOutput, calls=%fused_computation | convolution fusion | flops 3223322624 | bytes 11272192 | tf_op jit(solution)/shard_map/dot_general | solution.py:35
  47.8 200.5 %reduce-scatter.7.cloned.1.call-done = bf16[40,3072]{1,0:T(8,128)(2,1)} async-done(((bf16[640,3072]{1,0:T(8,128)(2,1)}), bf16[40,3072]{1,0:T(8,128)(2,1)}) %reduce-scatter.7.cloned.1.call-update) | async-done | bytes 245776
  248.3 1.2 fusion.22
  249.5 0.8 pad_maximum_fusion
  250.4 208.8 %reduce-scatter.5.cloned.1.call-done = bf16[32,4096]{1,0:T(8,128)(2,1)} async-done(((bf16[512,4096]{1,0:T(8,128)(2,1)}), bf16[32,4096]{1,0:T(8,128)(2,1)}) %reduce-scatter.5.cloned.1.call-update) | async-done | bytes 262160 | tf_op jit(solution)/shard_map/reduce_scatter | solution.py:34
  459.2 1.1 fusion.6
  460.3 1.3 multiply_reduce_fusion
  461.6 133.7 %all-gather.2.cloned.1.call-done = bf16[640,2,2,1536]{3,0,1,2:T(8,128)(2,1)} async-done(((bf16[40,2,2,1536]{3,0,1,2:T(8,128)(2,1)}), bf16[640,2,2,1536]{3,0,1,2:T(8,128)(2,1)}) %all-gather.2.cloned.1.call-update) | async-done | bytes 7864336 | tf_op jit(solution)/shard_map/all_gather | solution.py:80
  595.2 3.9 fusion
  599.2 0.9 copy-done.5
  600.1 2.7 fusion.5
  602.8 1.5 copy.44
  604.3 5.4 all-to-all-start.1
  609.7 1.0 fusion.20
  610.6 10.4 %all-to-all-done.1 = bf16[640,2,256]{2,1,0:T(2,128)(2,1)S(1)} async-done(((bf16[640,2,256]{2,1,0:T(2,128)(2,1)}), bf16[640,2,256]{2,1,0:T(2,128)(2,1)S(1)}, u32[]{:S(2)}, u32[]{:S(2)}) %all-to-all-start.1) | async-done | bytes 655392 | tf_op jit(solution)/shard_map/all_to_all | solution.py:88
  621.1 0.7 copy.58
  621.8 0.3 reshape.44
  622.0 1.9 fusion.23
  (23 shorter events, 0.3 us)
Async XLA Ops:
  7.2 28.0 %copy-start = (bf16[2,1536,256]{2,1,0:T(8,128)(2,1)S(1)}, bf16[2,1536,256]{2,1,0:T(8,128)(2,1)}, u32[]{:S(2)}) copy-start(bf16[2,1536,256]{2,1,0:T(8,128)(2,1)} %param.21) | copy-start | bytes 4718596
  7.2 241.1 %reduce-scatter.7.cloned.1.call-start = ((), (), s32[]{:S(2)}) async-start(), calls=%async_computation.6 | async-start | bytes 4177920
  38.9 1.1 copy-start.6
  38.9 420.3 %reduce-scatter.5.cloned.1.call-start = ((), (), s32[]{:S(2)}) async-start(), calls=%async_computation.4 | async-start | bytes 4456448 | tf_op jit(solution)/shard_map/reduce_scatter | solution.py:34
  47.8 200.5 %copy-start.3 = (bf16[40,2,1536]{2,1,0:T(2,128)(2,1)S(1)}, bf16[40,2,1536]{2,1,0:T(2,128)(2,1)}, u32[]{:S(2)}) copy-start(bf16[40,2,1536]{2,1,0:T(2,128)(2,1)} %param.18) | copy-start | bytes 737284
  47.8 200.5 %copy-start.4 = (bf16[40,2,1536]{2,1,0:T(2,128)(2,1)S(1)}, bf16[40,2,1536]{2,1,0:T(2,128)(2,1)}, u32[]{:S(2)}) copy-start(bf16[40,2,1536]{2,1,0:T(2,128)(2,1)} %param.17) | copy-start | bytes 737284
  47.8 411.4 %copy-start.1 = (f32[32,4096]{1,0:T(8,128)S(1)}, f32[32,4096]{1,0:T(8,128)}, u32[]{:S(2)}) copy-start(f32[32,4096]{1,0:T(8,128)} %param.13) | copy-start | bytes 1572868
  47.8 547.4 %all-gather.2.cloned.1.call-start = ((), (), s32[]{:S(2)}) async-start(), calls=%async_computation.5 | async-start | bytes 8355840 | tf_op jit(solution)/shard_map/all_gather | solution.py:80
  595.2 4.9 copy-start.5
  600.1 9.6 %copy-start.2 = (bf16[32,4096]{1,0:T(8,128)(2,1)S(1)}, bf16[32,4096]{1,0:T(8,128)(2,1)}, u32[]{:S(2)}) copy-start(bf16[32,4096]{1,0:T(8,128)(2,1)} %reduce-scatter.5.cloned.1.call-done) | copy-start | bytes 786436
  604.3 16.8 %all-to-all-start.1 = ((bf16[640,2,256]{2,1,0:T(2,128)(2,1)}), bf16[640,2,256]{2,1,0:T(2,128)(2,1)S(1)}, u32[]{:S(2)}, u32[]{:S(2)}) async-start(bf16[640,2,256]{2,1,0:T(2,128)(2,1)} %copy.44), calls=%async_computation.2 | async-start | bytes 1310720 | tf_op jit(solution)/shard_map/all_to_all | solution.py:88
Sparse Core Ops, SparseCore 0:
  39.0 209.2 reduce-scatter.6
  252.8 206.2 reduce-scatter.4
  462.3 132.8 all-gather.1
where the time goes:
time: 631 us; the launch traced here: 630 us
  waiting for transfers between devices  553 us (88%)
  matrix products  19.1 us (3%)
  blocking collectives  18.3 us (3%)
  between operations  13.8 us (2%)
  other arithmetic  12 us (2%)
  local copies, waits for them, and re-layouts  8.38 us (1%)
    reduce_scatter x1, waiting for transfers between devices, weight_update(): lax.psum_scatter(lax.dot_general(query_grad, attn_input, (((0,), (0,)), (...  209 us
    unnamed x4, waiting for transfers between devices  200 us
    all_gather x1, waiting for transfers between devices, expert_update(): part_rows = lax.all_gather(grads_pair, 'dp', axis=0, tiled=True)  134 us
    all_to_all x1, blocking collectives, expert_update(): lax.all_to_all(outgoing, 'expert', split_axis=1, concat_axis=0, tiled=True)  18.3 us
  transfers between devices with their start and end apart: 4, of which 4 were waited for; matrix products, arithmetic and copies ran while one was open for 2% of the time, Pallas kernels for 0%

commit v1 on v0

--- a/solution.py
+++ b/solution.py
@@ -11,7 +11,15 @@
     expert_iota = lax.broadcasted_iota(jnp.int32, (1, 1, experts), 2)
     chosen = (expert_ids[:, :, None] == expert_iota).astype(jnp.int32)
     counts = jnp.sum(chosen, axis=1, dtype=jnp.int32)
-    before = jnp.cumsum(counts, axis=0, dtype=jnp.int32) - counts
+    rows = counts.shape[0]
+    earlier = lax.broadcasted_iota(jnp.int32, (rows, rows), 1) < lax.broadcasted_iota(
+        jnp.int32, (rows, rows), 0
+    )
+    before = jnp.dot(
+        earlier.astype(jnp.bfloat16),
+        counts.astype(jnp.bfloat16),
+        preferred_element_type=jnp.float32,
+    ).astype(jnp.int32)
     position = jnp.sum(chosen * before[:, None, :], axis=2, dtype=jnp.int32)
     slot_code = position * experts + expert_ids
     slot_iota = lax.broadcasted_iota(jnp.int32, (1, 1, capacity * experts), 2)

time: 631 us -> 631 us (level)
  no operation moved by 1% of the time
where the time goes in v1:
time: 631 us; the launch traced here: 630 us
  waiting for transfers between devices  553 us (88%)
  matrix products  19.2 us (3%)
  blocking collectives  18.3 us (3%)
  between operations  13.8 us (2%)
  other arithmetic  11.8 us (2%)
  local copies, waits for them, and re-layouts  8.22 us (1%)
    reduce_scatter x1, waiting for transfers between devices, weight_update(): lax.psum_scatter(lax.dot_general(query_grad, attn_input, (((0,), (0,)), (...  209 us
    unnamed x4, waiting for transfers between devices  201 us
    all_gather x1, waiting for transfers between devices, expert_update(): part_rows = lax.all_gather(grads_pair, 'dp', axis=0, tiled=True)  134 us
    all_to_all x1, blocking collectives, expert_update(): lax.all_to_all(outgoing, 'expert', split_axis=1, concat_axis=0, tiled=True)  18.3 us
  transfers between devices with their start and end apart: 4, of which 4 were waited for; matrix products, arithmetic and copies ran while one was open for 2% of the time, Pallas kernels for 0%

profile of v1, /device:TPU:1, one launch (start us, length us, event | category | flops | bytes accessed | tf_op | source)
XLA Modules:
  0.0 630.1 jit_solution(1963007149182575208)
XLA Ops:
  7.2 0.8 convert_reduce_fusion.1
  8.0 0.1 convolution_convert_fusion.3
  8.2 0.7 select_reduce_fusion.1
  8.9 0.7 multiply_add_fusion
  9.6 0.1 copy.38
  9.7 0.8 copy.39
  10.5 4.1 convert_reduce_fusion
  14.6 1.6 convolution_convert_fusion.2
  16.2 0.4 copy.40
  16.6 18.3 %all_to_all.33 = bf16[40,32,256]{2,0,1:T(8,128)(2,1)S(1)} all-to-all(bf16[40,32,256]{2,0,1:T(8,128)(2,1)S(1)} %copy.40), channel_id=1, replica_groups=mesh['expert'=16,'dp'=16] {'expert'}, dimensions={1} | all-to-all | bytes 1310720 | tf_op jit(solution)/shard_map/all_to_all | solution.py:78
  35.0 1.2 fusion.2
  36.2 2.5 copy.49
  38.7 0.0 reduce-scatter.5.cloned.1.call-start
  38.7 1.1 copy-done.6
  39.8 7.8 %convolution_convert_fusion = bf16[512,4096]{1,0:T(8,128)(2,1)} fusion(bf16[768,512]{1,0:T(8,128)(2,1)S(1)} %copy-done.6, bf16[768,4096]{1,0:T(8,128)(2,1)} %param.11), kind=kOutput, calls=%fused_computation | convolution fusion | flops 3223322624 | bytes 11272192 | tf_op jit(solution)/shard_map/dot_general | solution.py:43
  47.6 200.5 %reduce-scatter.7.cloned.1.call-done = bf16[40,3072]{1,0:T(8,128)(2,1)} async-done(((bf16[640,3072]{1,0:T(8,128)(2,1)}), bf16[40,3072]{1,0:T(8,128)(2,1)}) %reduce-scatter.7.cloned.1.call-update) | async-done | bytes 245776
  248.1 1.2 fusion.22
  249.3 0.8 pad_maximum_fusion
  250.2 208.7 %reduce-scatter.5.cloned.1.call-done = bf16[32,4096]{1,0:T(8,128)(2,1)} async-done(((bf16[512,4096]{1,0:T(8,128)(2,1)}), bf16[32,4096]{1,0:T(8,128)(2,1)}) %reduce-scatter.5.cloned.1.call-update) | async-done | bytes 262160 | tf_op jit(solution)/shard_map/reduce_scatter | solution.py:42
  458.8 1.1 fusion.6
  460.0 1.3 multiply_reduce_fusion
  461.3 133.7 %all-gather.2.cloned.1.call-done = bf16[640,2,2,1536]{3,0,1,2:T(8,128)(2,1)} async-done(((bf16[40,2,2,1536]{3,0,1,2:T(8,128)(2,1)}), bf16[640,2,2,1536]{3,0,1,2:T(8,128)(2,1)}) %all-gather.2.cloned.1.call-update) | async-done | bytes 7864336 | tf_op jit(solution)/shard_map/all_gather | solution.py:88
  594.9 3.9 fusion
  598.9 0.9 copy-done.5
  599.8 2.7 fusion.5
  602.5 1.5 copy.44
  604.0 5.4 all-to-all-start.1
  609.3 1.0 fusion.20
  610.3 10.4 %all-to-all-done.1 = bf16[640,2,256]{2,1,0:T(2,128)(2,1)S(1)} async-done(((bf16[640,2,256]{2,1,0:T(2,128)(2,1)}), bf16[640,2,256]{2,1,0:T(2,128)(2,1)S(1)}, u32[]{:S(2)}, u32[]{:S(2)}) %all-to-all-start.1) | async-done | bytes 655392 | tf_op jit(solution)/shard_map/all_to_all | solution.py:96
  620.8 0.7 copy.58
  621.5 0.3 reshape.36
  621.7 1.9 fusion.24
  (20 shorter events, 0.2 us)
Async XLA Ops:
  7.2 27.8 %copy-start = (bf16[2,1536,256]{2,1,0:T(8,128)(2,1)S(1)}, bf16[2,1536,256]{2,1,0:T(8,128)(2,1)}, u32[]{:S(2)}) copy-start(bf16[2,1536,256]{2,1,0:T(8,128)(2,1)} %param.21) | copy-start | bytes 4718596
  7.2 240.9 %reduce-scatter.7.cloned.1.call-start = ((), (), s32[]{:S(2)}) async-start(), calls=%async_computation.6 | async-start | bytes 4177920
  38.7 1.1 copy-start.6
  38.7 420.2 %reduce-scatter.5.cloned.1.call-start = ((), (), s32[]{:S(2)}) async-start(), calls=%async_computation.4 | async-start | bytes 4456448 | tf_op jit(solution)/shard_map/reduce_scatter | solution.py:42
  47.6 200.5 %copy-start.3 = (bf16[40,2,1536]{2,1,0:T(2,128)(2,1)S(1)}, bf16[40,2,1536]{2,1,0:T(2,128)(2,1)}, u32[]{:S(2)}) copy-start(bf16[40,2,1536]{2,1,0:T(2,128)(2,1)} %param.18) | copy-start | bytes 737284
  47.6 200.5 %copy-start.4 = (bf16[40,2,1536]{2,1,0:T(2,128)(2,1)S(1)}, bf16[40,2,1536]{2,1,0:T(2,128)(2,1)}, u32[]{:S(2)}) copy-start(bf16[40,2,1536]{2,1,0:T(2,128)(2,1)} %param.17) | copy-start | bytes 737284
  47.6 411.3 %copy-start.1 = (f32[32,4096]{1,0:T(8,128)S(1)}, f32[32,4096]{1,0:T(8,128)}, u32[]{:S(2)}) copy-start(f32[32,4096]{1,0:T(8,128)} %param.13) | copy-start | bytes 1572868
  47.6 547.3 %all-gather.2.cloned.1.call-start = ((), (), s32[]{:S(2)}) async-start(), calls=%async_computation.5 | async-start | bytes 8355840 | tf_op jit(solution)/shard_map/all_gather | solution.py:88
  594.9 4.9 copy-start.5
  599.8 9.6 %copy-start.2 = (bf16[32,4096]{1,0:T(8,128)(2,1)S(1)}, bf16[32,4096]{1,0:T(8,128)(2,1)}, u32[]{:S(2)}) copy-start(bf16[32,4096]{1,0:T(8,128)(2,1)} %reduce-scatter.5.cloned.1.call-done) | copy-start | bytes 786436
  604.0 16.8 %all-to-all-start.1 = ((bf16[640,2,256]{2,1,0:T(2,128)(2,1)}), bf16[640,2,256]{2,1,0:T(2,128)(2,1)S(1)}, u32[]{:S(2)}, u32[]{:S(2)}) async-start(bf16[640,2,256]{2,1,0:T(2,128)(2,1)} %copy.44), calls=%async_computation.2 | async-start | bytes 1310720 | tf_op jit(solution)/shard_map/all_to_all | solution.py:96
Sparse Core Ops, SparseCore 0:
  38.8 209.2 reduce-scatter.6
  252.6 206.1 reduce-scatter.4
  462.0 132.8 all-gather.1

commit v2 on v0

v2 whole, which is shorter than its diff:
```python
import functools

import jax
import jax.numpy as jnp
from jax import lax
from jax.experimental import pallas as pl
from jax.experimental.pallas import tpu as pltpu
from jax.sharding import PartitionSpec as P

STEP_RATE = 0.01
EPSILON = 1e-06
MESH = pl.DeviceIdType.MESH
NZ = 8
NE = 16
LANES = 4
NT = (((1,), (1,)), ((), ()))
BF = jnp.bfloat16
F32 = jnp.float32


def remote(src, dst, send_sem, recv_sem, device):
    return pltpu.make_async_remote_copy(
        src_ref=src,
        dst_ref=dst,
        send_sem=send_sem,
        recv_sem=recv_sem,
        device_id=device,
        device_id_type=MESH,
    )


def sign(lane):
    return 1 if lane < 2 else -1


def step_kernel(
    ids_ref,
    route_ref,
    cot_ref,
    grad_hbm,
    input_hbm,
    weight_hbm,
    gate_hbm,
    up_hbm,
    gate_w_hbm,
    up_w_hbm,
    down_w_hbm,
    query_out,
    moe_out,
    grad_v,
    grad_t,
    input_v,
    weight_v,
    gate_v,
    up_v,
    gate_w,
    up_w,
    down_w,
    onehot,
    outgoing,
    arrived,
    q_part,
    q_recv,
    q_give,
    q_take,
    h_part,
    h_recv,
    h_give,
    h_take,
    grads,
    result,
    returned,
    load_sem,
    disp_send,
    disp_recv,
    q_send,
    q_got,
    qx_send,
    qx_got,
    h_send,
    h_got,
    hx_send,
    hx_got,
    g_send,
    g_got,
    gx_send,
    gx_got,
    r_send,
    r_got,
):
    e = lax.axis_index("expert")
    d = lax.axis_index("dp")
    h = d // NZ
    z = lax.rem(d, NZ)
    twin = (e, (1 - h) * NZ + z)
    ahead = (e, h * NZ + lax.rem(z + 1, NZ))
    behind = (e, h * NZ + lax.rem(z + NZ - 1, NZ))

    def toward(lane):
        return ahead if sign(lane) > 0 else behind

    def at_z(lane, hops):
        return lax.rem(z + 4 * NZ - sign(lane) * hops, NZ)

    loads = [
        pltpu.make_async_copy(src, dst, load_sem.at[i])
        for i, (src, dst) in enumerate(
            (
                (grad_hbm, grad_v),
                (input_hbm, input_v),
                (down_w_hbm, down_w),
                (gate_hbm, gate_v),
                (up_hbm, up_v),
                (gate_w_hbm, gate_w),
                (up_w_hbm, up_w),
                (weight_hbm, weight_v),
            )
        )
    ]
    for copy in loads:
        copy.start()

    barrier = pltpu.get_barrier_semaphore()

    @pl.loop(1, NE)
    def _(k):
        pl.semaphore_signal(
            barrier, inc=1, device_id=(lax.rem(e + k, NE), d), device_id_type=MESH
        )

    for device in (ahead, behind, twin):
        pl.semaphore_signal(barrier, inc=1, device_id=device, device_id_type=MESH)

    experts = 2 * NE
    tokens = ids_ref.shape[1]
    slots = outgoing.shape[1]
    which = lax.broadcasted_iota(jnp.int32, (experts, tokens), 0)
    chosen = jnp.zeros((experts, tokens), F32)
    share = jnp.zeros((experts, tokens), F32)
    for k in range(ids_ref.shape[0]):
        hit = ids_ref[k : k + 1, :] == which
        chosen = chosen + jnp.where(hit, 1.0, 0.0)
        share = share + jnp.where(hit, route_ref[k : k + 1, :], 0.0)
    earlier = lax.broadcasted_iota(jnp.int32, (tokens, tokens), 0) < lax.broadcasted_iota(
        jnp.int32, (tokens, tokens), 1
    )
    before = jnp.dot(
        chosen.astype(BF), jnp.where(earlier, 1.0, 0.0).astype(BF), preferred_element_type=F32
    )
    position = jnp.where(chosen > 0.5, before, -1.0).astype(jnp.int32)
    slot_iota = lax.broadcasted_iota(jnp.int32, (slots, tokens), 0)
    cot = cot_ref[...]
    for block in range(experts):
        mine = position[block : block + 1, :] == slot_iota
        scale = jnp.sum(
            jnp.where(mine, share[block : block + 1, :], 0.0), axis=1, keepdims=True
        )
        pick = jnp.where(mine, 1.0, 0.0).astype(BF)
        onehot[block] = pick
        rows = jnp.dot(pick, cot, preferred_element_type=F32)
        outgoing[block] = (rows * scale).astype(BF)

    pl.semaphore_wait(barrier, NE + 2)

    def dispatch(k):
        to = lax.rem(e + k, NE)
        return remote(
            outgoing.at[pl.ds(2 * to, 2)],
            arrived.at[:, e],
            disp_send.at[k],
            disp_recv.at[k],
            (to, d),
        )

    @pl.loop(1, NE)
    def _(k):
        dispatch(k).start()

    arrived[:, e] = outgoing[pl.ds(2 * e, 2)]

    def ring(part, recv, send, got, lane, t):
        src = part.at[lane, :, at_z(lane, 1)] if isinstance(t, int) else recv.at[lane, t - 1]
        return remote(src, recv.at[lane, t], send.at[lane, t], got.at[lane, t], toward(lane))

    def await_step(recv, send, got, lane, t):
        at = recv.at[lane, t]
        remote(at, at, send.at[lane, t], got.at[lane, t], toward(lane)).wait_recv()

    def forward(part, recv, send, got, lane, t):
        await_step(recv, send, got, lane, t - 1)
        total = recv[lane, t - 1].astype(F32) + part[lane, :, at_z(lane, 1 + t)].astype(F32)
        recv[lane, t - 1] = total.astype(BF)
        ring(part, recv, send, got, lane, t).start()

    loads[0].wait()
    loads[1].wait()
    grad_t[...] = grad_v[...].T
    q_wide = q_part.shape[-1]
    for lane in range(LANES):

        @pl.loop(0, q_wide // 256)
        def _(j):
            columns = pl.ds(pl.multiple_of(lane * q_wide + j * 256, 256), 256)
            part = jnp.dot(grad_t[...], input_v[:, columns], preferred_element_type=F32)
            q_part[lane, :, :, :, pl.ds(pl.multiple_of(j * 256, 256), 256)] = part.astype(
                BF
            ).reshape(2, NZ, 32, 256)

        ring(q_part, q_recv, q_send, q_got, lane, 0).start()

    @pl.loop(1, NE)
    def _(k):
        dispatch(k).wait_recv()

    loads[2].wait()
    h_wide = h_part.shape[-1]
    for lane in range(LANES):
        expert, half = lane // 2, lane % 2

        @pl.loop(0, h_wide // 256)
        def _(j):
            rows = pl.ds(pl.multiple_of(half * h_wide + j * 256, 256), 256)
            part = lax.dot_general(
                arrived[expert].reshape(NE * slots, -1),
                down_w[expert, rows, :],
                NT,
                preferred_element_type=F32,
            )
            h_part[lane, :, :, :, pl.ds(pl.multiple_of(j * 256, 256), 256)] = part.astype(
                BF
            ).reshape(2, NZ, slots, 256)

        ring(h_part, h_recv, h_send, h_got, lane, 0).start()

    @pl.loop(1, NZ - 1)
    def _(t):
        for lane in range(LANES):
            forward(q_part, q_recv, q_send, q_got, lane, t)
        for lane in range(LANES):
            forward(h_part, h_recv, h_send, h_got, lane, t)

    last = NZ - 2

    def exchange(give, take, send, got, lane):
        return remote(give.at[lane], take.at[lane], send.at[lane], got.at[lane], twin)

    def settle(part, recv, send, got, give, take, x_send, x_got, lane):
        await_step(recv, send, got, lane, last)
        theirs = recv[lane, last, 1 - h].astype(F32) + part[lane, 1 - h, z].astype(F32)
        give[lane] = theirs.astype(BF)
        exchange(give, take, x_send, x_got, lane).start()

    def total_of(part, recv, give, take, x_send, x_got, lane):
        exchange(give, take, x_send, x_got, lane).wait_recv()
        mine = recv[lane, last, h].astype(F32) + part[lane, h, z].astype(F32)
        return mine + take[lane].astype(F32)

    for lane in range(LANES):
        settle(h_part, h_recv, h_send, h_got, h_give, h_take, hx_send, hx_got, lane)
    for i in (3, 4, 5, 6, 7):
        loads[i].wait()

    def gather(lane, chain, t):
        side = h if chain == 0 else 1 - h
        at = grads.at[lane, side, at_z(lane, t)]
        return remote(at, at, g_send.at[lane, chain, t], g_got.at[lane, chain, t], toward(lane))

    def swap(lane):
        at = grads.at[lane, h, z]
        return remote(at, at, gx_send.at[lane], gx_got.at[lane], twin)

    for expert in range(2):
        for half in range(2):
            lane = 2 * expert + half
            hidden = total_of(h_part, h_recv, h_give, h_take, hx_send, hx_got, lane)
            columns = slice(half * h_wide, (half + 1) * h_wide)
            g = gate_v[:, expert, columns].astype(F32)
            u = up_v[:, expert, columns].astype(F32)
            sigma = 1.0 / (1.0 + jnp.exp(-g))
            grads[2 * expert, h, z, :, columns] = (
                hidden * u * sigma * (1.0 + g * (1.0 - sigma))
            ).astype(BF)
            grads[2 * expert + 1, h, z, :, columns] = (hidden * g * sigma).astype(BF)
        for lane in (2 * expert, 2 * expert + 1):
            gather(lane, 0, 0).start()
            swap(lane).start()

    for lane in range(LANES):
        remote_in = swap(lane)
        remote_in.wait_recv()
        gather(lane, 1, 0).start()
    for lane in range(LANES):
        settle(q_part, q_recv, q_send, q_got, q_give, q_take, qx_send, qx_got, lane)

    def reply(expert, side, block):
        to = side * NZ + block
        return remote(
            result.at[expert, side, block],
            returned.at[e, expert],
            r_send.at[expert, side, block],
            r_got.at[e, expert],
            (to, d),
        )

    def produce(expert, block):
        gate = grads[2 * expert, :, block].reshape(2 * slots, -1)
        up = grads[2 * expert + 1, :, block].reshape(2 * slots, -1)
        rows = lax.dot_general(gate, gate_w[expert], NT, preferred_element_type=F32)
        rows = rows + lax.dot_general(up, up_w[expert], NT, preferred_element_type=F32)
        rows = rows.astype(BF).reshape(2, slots, -1)
        for side in range(2):
            result[expert, side, block] = rows[side]
            to = side * NZ + block

            @pl.when(to == e)
            def _():
                returned[e, expert] = rows[side]

            @pl.when(to != e)
            def _():
                reply(expert, side, block).start()

    for expert in range(2):
        produce(expert, z)

    @pl.loop(0, NZ - 1)
    def _(t):
        for lane in range(LANES):
            for chain in range(2):
                gather(lane, chain, t).wait_recv()

                @pl.when(t < NZ - 2)
                def _():
                    gather(lane, chain, t + 1).start()

        for expert in range(2):
            produce(expert, at_z(2 * expert, t + 1))

    for lane in range(LANES):
        columns = slice(lane * q_wide, (lane + 1) * q_wide)
        query_out[:, columns] = total_of(
            q_part, q_recv, q_give, q_take, qx_send, qx_got, lane
        )
    gradient = query_out[...]
    weight = weight_v[...]
    count = 1.0 / weight.shape[1]
    radial = (jnp.sum(weight * gradient, axis=1, keepdims=True) * count) / (
        jnp.sum(weight * weight, axis=1, keepdims=True) * count + EPSILON
    )
    stepped = weight - STEP_RATE * (gradient - radial * weight)
    norm = jnp.sum(stepped * stepped, axis=1, keepdims=True) * count + EPSILON
    query_out[...] = stepped * lax.rsqrt(norm)

    @pl.loop(1, NE)
    def _(k):
        source = lax.rem(e + k, NE)
        for expert in range(2):
            at = returned.at[source, expert]
            remote(
                at, at, r_send.at[expert, 0, 0], r_got.at[source, expert], twin
            ).wait_recv()

    moe_out[...] = lax.dot_general(
        onehot[...].reshape(experts * slots, tokens),
        returned[...].reshape(experts * slots, -1),
        (((0,), (0,)), ((), ())),
        preferred_element_type=F32,
    )

    @pl.loop(1, NE)
    def _(k):
        dispatch(k).wait_send()

    for lane in range(LANES):
        ring(q_part, q_recv, q_send, q_got, lane, 0).wait_send()
        ring(h_part, h_recv, h_send, h_got, lane, 0).wait_send()
        exchange(q_give, q_take, qx_send, qx_got, lane).wait_send()
        exchange(h_give, h_take, hx_send, hx_got, lane).wait_send()
        swap(lane).wait_send()

    @pl.loop(1, NZ - 1)
    def _(t):
        for lane in range(LANES):
            ring(q_part, q_recv, q_send, q_got, lane, t).wait_send()
            ring(h_part, h_recv, h_send, h_got, lane, t).wait_send()

    @pl.loop(0, NZ - 1)
    def _(t):
        for lane in range(LANES):
            for chain in range(2):
                gather(lane, chain, t).wait_send()

    @pl.loop(0, NZ)
    def _(block):
        for side in range(2):

            @pl.when(side * NZ + block != e)
            def _():
                for expert in range(2):
                    reply(expert, side, block).wait_send()


def shards(
    attn_input,
    query_grad,
    query_weight,
    moe_cotangent,
    expert_ids,
    route_weights,
    gate_saved,
    up_saved,
    gate_weight,
    up_weight,
    down_weight,
):
    vmem = pl.BlockSpec(memory_space=pltpu.VMEM)
    hbm = pl.BlockSpec(memory_space=pl.ANY)
    dma = pltpu.SemaphoreType.DMA
    tokens, width = moe_cotangent.shape
    slots, local, hidden = gate_saved.shape
    rows, model = query_weight.shape
    batch, heads = query_grad.shape
    q_wide, h_wide = model // LANES, local * hidden // LANES
    scratch = [
        pltpu.VMEM(query_grad.shape, BF),
        pltpu.VMEM((heads, batch), BF),
        pltpu.VMEM(attn_input.shape, BF),
        pltpu.VMEM(query_weight.shape, F32),
        pltpu.VMEM(gate_saved.shape, BF),
        pltpu.VMEM(up_saved.shape, BF),
        pltpu.VMEM(gate_weight.shape, BF),
        pltpu.VMEM(up_weight.shape, BF),
        pltpu.VMEM(down_weight.shape, BF),
        pltpu.VMEM((local * NE, slots, tokens), BF),
        pltpu.VMEM((local * NE, slots, width), BF),
        pltpu.VMEM((local, NE, slots, width), BF),
        pltpu.VMEM((LANES, 2, NZ, rows, q_wide), BF),
        pltpu.VMEM((LANES, NZ - 1, 2, rows, q_wide), BF),
        pltpu.VMEM((LANES, rows, q_wide), BF),
        pltpu.VMEM((LANES, rows, q_wide), BF),
        pltpu.VMEM((LANES, 2, NZ, slots, h_wide), BF),
        pltpu.VMEM((LANES, NZ - 1, 2, slots, h_wide), BF),
        pltpu.VMEM((LANES, slots, h_wide), BF),
        pltpu.VMEM((LANES, slots, h_wide), BF),
        pltpu.VMEM((LANES, 2, NZ, slots, hidden), BF),
        pltpu.VMEM((local, 2, NZ, slots, width), BF),
        pltpu.VMEM((NE, local, slots, width), BF),
        dma((8,)),
        dma((NE,)),
        dma((NE,)),
        dma((LANES, NZ - 1)),
        dma((LANES, NZ - 1)),
        dma((LANES,)),
        dma((LANES,)),
        dma((LANES, NZ - 1)),
        dma((LANES, NZ - 1)),
        dma((LANES,)),
        dma((LANES,)),
        dma((LANES, 2, NZ - 1)),
        dma((LANES, 2, NZ - 1)),
        dma((LANES,)),
        dma((LANES,)),
        dma((local, 2, NZ)),
        dma((NE, local)),
    ]
    return pl.pallas_call(
        step_kernel,
        name="backward_step",
        out_shape=(
            jax.ShapeDtypeStruct((rows, model), F32),
            jax.ShapeDtypeStruct((tokens, width), F32),
        ),
        in_specs=[vmem, vmem, vmem] + [hbm] * 8,
        out_specs=(vmem, vmem),
        scratch_shapes=scratch,
        compiler_params=pltpu.CompilerParams(
            collective_id=0, has_side_effects=True, vmem_limit_bytes=58 << 20
        ),
    )(
        expert_ids.T,
        route_weights.T,
        moe_cotangent,
        query_grad,
        attn_input,
        query_weight,
        gate_saved,
        up_saved,
        gate_weight,
        up_weight,
        down_weight,
    )


def solution(mesh):
    placed = (
        P("dp", None),
        P("dp", "expert"),
        P(("expert", "dp"), None),
        P("expert", "dp"),
        P("expert", None),
        P("expert", None),
        P("dp", "expert", None),
        P("dp", "expert", None),
        P("expert", "dp", None),
        P("expert", "dp", None),
        P("expert", None, "dp"),
    )
    return jax.shard_map(
        shards,
        mesh=mesh,
        in_specs=placed,
        out_specs=(P(("expert", "dp"), None), P("expert", "dp")),
        check_vma=False,
    )
```

time: 631 us -> 192 us (0.30)
  waiting for transfers between devices: 553 us -> 0 us
  Pallas kernels: 0 us -> 188 us
  matrix products: 19.1 us -> 0 us
  blocking collectives: 18.3 us -> 0 us
  between operations: 13.8 us -> 0.64 us
  other arithmetic: 12 us -> 0 us
    reduce_scatter x1 -> x0, waiting for transfers between devices: 209 us -> none  [weight_update(): lax.psum_scatter(lax.dot_general(query_grad, attn_input, (((0,), (0,)), (...]
    unnamed x4 -> x0, waiting for transfers between devices: 200 us -> none
    pallas_call x0 -> x1, Pallas kernels: none -> 188 us  [shards(): pl.pallas_call(step_kernel, name='backward_step', out_shape=(jax.ShapeDty...]
    all_gather x1 -> x0, waiting for transfers between devices: 134 us -> none  [expert_update(): part_rows = lax.all_gather(grads_pair, 'dp', axis=0, tiled=True)]
    dot_general x6 -> x0, matrix products: 19.1 us -> none  [the longest x1 7.78 us: weight_update(): lax.dot_general(query_grad, attn_input, (((0,), (0,)), ((), ())), preferr...]
    all_to_all x1 -> x0, blocking collectives: 18.3 us -> none  [expert_update(): lax.all_to_all(outgoing, 'expert', split_axis=1, concat_axis=0, tiled=True)]
    all_to_all x1 -> x0, waiting for transfers between devices: 10.4 us -> none  [expert_update(): lax.all_to_all(slot_input, 'expert', split_axis=0, concat_axis=1, tiled=T...]
    reduce_sum x5 -> x0, other arithmetic: 8.07 us -> none  [the longest x1 4.13 us: slot_tables(): select = jnp.sum(matched.astype(jnp.float32), axis=1)]
  transfers between devices with their start and end apart: 4 -> 0, of which waited for: 4 -> 0; matrix products, arithmetic and copies ran while one was open for 2% -> 0% of each run, Pallas kernels for 0% -> 0%
where the time goes in v2:
time: 192 us
  Pallas kernels  188 us (98%)
  local copies, waits for them, and re-layouts  3.44 us (2%)
    pallas_call x1, Pallas kernels, shards(): pl.pallas_call(step_kernel, name='backward_step', out_shape=(jax.ShapeDty...  188 us

profile of v2, /device:TPU:1, one launch (start us, length us, event | category | flops | bytes accessed | tf_op | source)
XLA Modules:
  0.0 192.3 jit_solution(13416608018178340776)
XLA Ops:
  0.6 188.2 %backward_step.1 = (f32[32,4096]{1,0:T(8,128)}, f32[128,256]{1,0:T(8,128)}) custom-call(s32[8,128]{1,0:T(8,128)} %bitcast.2, f32[8,128]{1,0:T(8,128)} %bitcast.3, bf16[128,256]{1,0:T(8,128)(2,1)} %cot_ref.1, bf16[768,512]{1,0:T(8,128)(2,1)} %grad_hbm.1, bf16[768,4096]{1,0:T(8,128)(2,1)} %input_hbm.1, f32[32,4096]{1,0:T(8,128)} %weight_hbm.1, ...), custom_call_target="tpu_custom_call" | custom-call | tf_op jit(solution)/shard_map/backward_step/pallas_call | solution.py:466
  188.9 1.9 copy.15
  190.7 1.6 copy.16

commit v3 on v2

v3 whole, which is shorter than its diff:
```python
import functools

import jax
import jax.numpy as jnp
from jax import lax
from jax.experimental import pallas as pl
from jax.experimental.pallas import tpu as pltpu
from jax.sharding import PartitionSpec as P

STEP_RATE = 0.01
EPSILON = 1e-06
MESH = pl.DeviceIdType.MESH
NZ = 8
NE = 16
LANES = 4
NT = (((1,), (1,)), ((), ()))
BF = jnp.bfloat16
F32 = jnp.float32


def remote(src, dst, send_sem, recv_sem, device):
    return pltpu.make_async_remote_copy(
        src_ref=src,
        dst_ref=dst,
        send_sem=send_sem,
        recv_sem=recv_sem,
        device_id=device,
        device_id_type=MESH,
    )


def sign(lane):
    return 1 if lane < 2 else -1


def step_kernel(
    ids_ref,
    route_ref,
    cot_ref,
    grad_hbm,
    input_hbm,
    weight_hbm,
    gate_hbm,
    up_hbm,
    gate_w_hbm,
    up_w_hbm,
    down_w_hbm,
    query_out,
    moe_out,
    grad_v,
    grad_t,
    input_v,
    weight_v,
    gate_v,
    up_v,
    gate_w,
    up_w,
    down_w,
    cot_in,
    onehot,
    scale,
    outgoing,
    arrived,
    q_part,
    q_recv,
    q_give,
    q_take,
    h_part,
    h_recv,
    grads,
    result,
    returned,
    load_sem,
    disp_send,
    disp_recv,
    pair_send,
    pair_got,
    q_send,
    q_got,
    qx_send,
    qx_got,
    h_send,
    h_got,
    g_send,
    g_got,
    r_send,
    r_got,
):
    e = lax.axis_index("expert")
    d = lax.axis_index("dp")
    h = d // NZ
    z = lax.rem(d, NZ)
    twin_d = (1 - h) * NZ + z
    twin = (e, twin_d)
    ahead = (e, h * NZ + lax.rem(z + 1, NZ))
    behind = (e, h * NZ + lax.rem(z + NZ - 1, NZ))
    units = gate_w.shape[-1]
    slots = gate_v.shape[1]
    experts = 2 * NE
    tokens = ids_ref.shape[1]

    def toward(lane):
        return ahead if sign(lane) > 0 else behind

    def at_z(lane, hops):
        return lax.rem(z + 4 * NZ - sign(lane) * hops, NZ)

    own = pl.ds(pl.multiple_of(h * units, 128), units)
    other = pl.ds(pl.multiple_of((1 - h) * units, 128), units)
    loads = [
        pltpu.make_async_copy(src, dst, load_sem.at[i])
        for i, (src, dst) in enumerate(
            (
                (grad_hbm, grad_v),
                (input_hbm, input_v),
                (down_w_hbm.at[:, h], down_w.at[h]),
                (gate_hbm.at[:, :, own], gate_v.at[h]),
                (up_hbm.at[:, :, own], up_v.at[h]),
                (gate_w_hbm.at[:, :, own], gate_w.at[h]),
                (up_w_hbm.at[:, :, own], up_w.at[h]),
                (weight_hbm, weight_v),
            )
        )
    ]
    shares = [
        remote(src, dst, pair_send.at[i], pair_got.at[i], twin)
        for i, (src, dst) in enumerate(
            (
                (cot_ref, cot_in),
                (down_w_hbm.at[:, 1 - h], down_w.at[h]),
                (gate_hbm.at[:, :, other], gate_v.at[h]),
                (up_hbm.at[:, :, other], up_v.at[h]),
                (gate_w_hbm.at[:, :, other], gate_w.at[h]),
                (up_w_hbm.at[:, :, other], up_w.at[h]),
            )
        )
    ]
    for copy in loads:
        copy.start()

    barrier = pltpu.get_barrier_semaphore()

    for device in (twin, ahead, behind):
        pl.semaphore_signal(barrier, inc=1, device_id=device, device_id_type=MESH)

    @pl.loop(1, NE)
    def _(k):
        for column in (d, twin_d):
            pl.semaphore_signal(
                barrier, inc=1, device_id=(lax.rem(e + k, NE), column), device_id_type=MESH
            )

    which = lax.broadcasted_iota(jnp.int32, (experts, tokens), 0)
    chosen = jnp.zeros((experts, tokens), F32)
    share = jnp.zeros((experts, tokens), F32)
    for k in range(ids_ref.shape[0]):
        hit = ids_ref[k : k + 1, :] == which
        chosen = chosen + jnp.where(hit, 1.0, 0.0)
        share = share + jnp.where(hit, route_ref[k : k + 1, :], 0.0)
    earlier = lax.broadcasted_iota(jnp.int32, (tokens, tokens), 0) < lax.broadcasted_iota(
        jnp.int32, (tokens, tokens), 1
    )
    before = jnp.dot(
        chosen.astype(BF), jnp.where(earlier, 1.0, 0.0).astype(BF), preferred_element_type=F32
    )
    position = jnp.where(chosen > 0.5, before, -1.0).astype(jnp.int32)
    slot_iota = lax.broadcasted_iota(jnp.int32, (slots, tokens), 0)
    for block in range(experts):
        mine = position[block : block + 1, :] == slot_iota
        scale[block] = jnp.sum(
            jnp.where(mine, share[block : block + 1, :], 0.0), axis=1, keepdims=True
        )
        onehot[block] = jnp.where(mine, 1.0, 0.0).astype(BF)

    def fill(side, cot):
        group = 8
        for first in range(0, experts, group):
            picks = onehot[first : first + group].reshape(group * slots, tokens)
            rows = jnp.dot(picks, cot, preferred_element_type=F32)
            rows = rows * scale[first : first + group].reshape(group * slots, 1)
            outgoing[side, first : first + group] = rows.astype(BF).reshape(group, slots, -1)

    fill(h, cot_ref[...])

    pl.semaphore_wait(barrier, 2 * NE + 1)
    shares[0].start()
    shares[1].start()

    def dispatch(side, k):
        to = lax.rem(e + k, NE)
        return remote(
            outgoing.at[side, pl.ds(2 * to, 2)],
            arrived.at[side, :, e],
            disp_send.at[side, k],
            disp_recv.at[side, k],
            (to, d),
        )

    def dispatch_all(side):
        @pl.loop(1, NE)
        def _(k):
            dispatch(side, k).start()

        arrived[side, :, e] = outgoing[side, pl.ds(2 * e, 2)]

    dispatch_all(h)
    shares[0].wait_recv()
    fill(1 - h, cot_in[...])
    dispatch_all(1 - h)

    def ring(part, recv, send, got, lane, t):
        src = part.at[lane, :, at_z(lane, 1)] if isinstance(t, int) else recv.at[lane, t - 1]
        return remote(src, recv.at[lane, t], send.at[lane, t], got.at[lane, t], toward(lane))

    def await_step(recv, send, got, lane, t):
        at = recv.at[lane, t]
        remote(at, at, send.at[lane, t], got.at[lane, t], toward(lane)).wait_recv()

    def forward(part, recv, send, got, t):
        for lane in range(LANES):
            await_step(recv, send, got, lane, t - 1)
            total = recv[lane, t - 1].astype(F32) + part[lane, :, at_z(lane, 1 + t)].astype(F32)
            recv[lane, t - 1] = total.astype(BF)
            ring(part, recv, send, got, lane, t).start()

    def q_forward(t):
        forward(q_part, q_recv, q_send, q_got, t)

    def h_forward(t):
        forward(h_part, h_recv, h_send, h_got, t)

    loads[0].wait()
    loads[1].wait()
    grad_t[...] = grad_v[...].T
    q_wide = q_part.shape[-1]
    for lane in range(LANES):

        @pl.loop(0, q_wide // 256)
        def _(j):
            columns = pl.ds(pl.multiple_of(lane * q_wide + j * 256, 256), 256)
            part = jnp.dot(grad_t[...], input_v[:, columns], preferred_element_type=F32)
            q_part[lane, :, :, :, pl.ds(pl.multiple_of(j * 256, 256), 256)] = part.astype(
                BF
            ).reshape(2, NZ, 32, 256)

        ring(q_part, q_recv, q_send, q_got, lane, 0).start()

    @pl.loop(1, 3)
    def _(t):
        q_forward(t)

    @pl.loop(1, NE)
    def _(k):
        for side in range(2):
            dispatch(side, k).wait_recv()

    loads[2].wait()
    shares[1].wait_recv()
    for copy in shares[2:]:
        copy.start()
    h_wide = h_part.shape[-1]
    for lane in range(LANES):
        expert, half = lane // 2, lane % 2
        rows = slice(half * h_wide, (half + 1) * h_wide)

        @pl.loop(0, 2)
        def _(block_side):
            part = 0.0
            for side in range(2):
                part = part + lax.dot_general(
                    arrived[side, expert, pl.ds(block_side * NZ, NZ)].reshape(NZ * slots, -1),
                    down_w[side, expert, rows, :],
                    NT,
                    preferred_element_type=F32,
                )
            h_part[lane, block_side] = part.astype(BF).reshape(NZ, slots, h_wide)

        ring(h_part, h_recv, h_send, h_got, lane, 0).start()

    @pl.loop(0, 3)
    def _(p):
        h_forward(2 * p + 1)
        h_forward(2 * p + 2)
        q_forward(p + 3)

    q_forward(jnp.int32(NZ - 2))
    last = NZ - 2

    def gather(lane, t):
        at = grads.at[lane, :, at_z(lane, t)]
        return remote(at, at, g_send.at[lane, t], g_got.at[lane, t], toward(lane))

    for i in (3, 4, 5, 6, 7):
        loads[i].wait()
    for i in (2, 3):
        shares[i].wait_recv()
    for expert in range(2):
        for half in range(2):
            lane = 2 * expert + half
            await_step(h_recv, h_send, h_got, lane, last)
            columns = slice(half * h_wide, (half + 1) * h_wide)
            for side in range(2):
                hidden = h_recv[lane, last, side].astype(F32) + h_part[lane, side, z].astype(F32)
                g = gate_v[side, :, expert, columns].astype(F32)
                u = up_v[side, :, expert, columns].astype(F32)
                sigma = 1.0 / (1.0 + jnp.exp(-g))
                grads[2 * expert, side, z, :, columns] = (
                    hidden * u * sigma * (1.0 + g * (1.0 - sigma))
                ).astype(BF)
                grads[2 * expert + 1, side, z, :, columns] = (hidden * g * sigma).astype(BF)
        for lane in (2 * expert, 2 * expert + 1):
            gather(lane, 0).start()

    def exchange(lane):
        return remote(q_give.at[lane], q_take.at[lane], qx_send.at[lane], qx_got.at[lane], twin)

    for lane in range(LANES):
        await_step(q_recv, q_send, q_got, lane, last)
        theirs = q_recv[lane, last, 1 - h].astype(F32) + q_part[lane, 1 - h, z].astype(F32)
        q_give[lane] = theirs.astype(BF)
        exchange(lane).start()

    def reply(expert, width, side, block):
        at = result.at[expert, width, side, block]
        return remote(
            at,
            returned.at[h, e, expert],
            r_send.at[expert, width, side, block],
            r_got.at[h, e, expert],
            (side * NZ + block, width * NZ + z),
        )

    def produce(expert, block):
        gate = grads[2 * expert, :, block].reshape(2 * slots, -1)
        up = grads[2 * expert + 1, :, block].reshape(2 * slots, -1)
        for width in range(2):
            rows = lax.dot_general(gate, gate_w[width, expert], NT, preferred_element_type=F32)
            rows = rows + lax.dot_general(
                up, up_w[width, expert], NT, preferred_element_type=F32
            )
            rows = rows.astype(BF).reshape(2, slots, -1)
            for side in range(2):
                result[expert, width, side, block] = rows[side]
                here = (side * NZ + block == e) & (width == h)

                @pl.when(here)
                def _():
                    returned[h, e, expert] = rows[side]

                @pl.when(jnp.logical_not(here))
                def _():
                    reply(expert, width, side, block).start()

    for i in (4, 5):
        shares[i].wait_recv()
    for expert in range(2):
        produce(expert, z)

    @pl.loop(0, NZ - 2)
    def _(t):
        for lane in range(LANES):
            gather(lane, t).wait_recv()
            gather(lane, t + 1).start()

        for expert in range(2):
            produce(expert, at_z(2 * expert, t + 1))

    for lane in range(LANES):
        exchange(lane).wait_recv()
        mine = q_recv[lane, last, h].astype(F32) + q_part[lane, h, z].astype(F32)
        query_out[:, lane * q_wide : (lane + 1) * q_wide] = mine + q_take[lane].astype(F32)
    gradient = query_out[...]
    weight = weight_v[...]
    count = 1.0 / weight.shape[1]
    radial = (jnp.sum(weight * gradient, axis=1, keepdims=True) * count) / (
        jnp.sum(weight * weight, axis=1, keepdims=True) * count + EPSILON
    )
    stepped = weight - STEP_RATE * (gradient - radial * weight)
    norm = jnp.sum(stepped * stepped, axis=1, keepdims=True) * count + EPSILON
    query_out[...] = stepped * lax.rsqrt(norm)

    for expert in range(2):
        for lane in (2 * expert, 2 * expert + 1):
            gather(lane, NZ - 2).wait_recv()
        produce(expert, at_z(2 * expert, NZ - 1))

    @pl.loop(0, NE)
    def _(source):
        for half in range(2):

            @pl.when(jnp.logical_not((source == e) & (half == h)))
            def _():
                for expert in range(2):
                    at = returned.at[half, source, expert]
                    remote(
                        at, at, r_send.at[expert, 0, 0, 0], r_got.at[half, source, expert], twin
                    ).wait_recv()

    total = 0.0
    for half in range(2):
        total = total + lax.dot_general(
            onehot[...].reshape(experts * slots, tokens),
            returned[half].reshape(experts * slots, -1),
            (((0,), (0,)), ((), ())),
            preferred_element_type=F32,
        )
    moe_out[...] = total

    for copy in shares:
        copy.wait_send()

    @pl.loop(1, NE)
    def _(k):
        for side in range(2):
            dispatch(side, k).wait_send()

    for lane in range(LANES):
        ring(q_part, q_recv, q_send, q_got, lane, 0).wait_send()
        ring(h_part, h_recv, h_send, h_got, lane, 0).wait_send()
        exchange(lane).wait_send()

    @pl.loop(1, NZ - 1)
    def _(t):
        for lane in range(LANES):
            ring(q_part, q_recv, q_send, q_got, lane, t).wait_send()
            ring(h_part, h_recv, h_send, h_got, lane, t).wait_send()

    @pl.loop(0, NZ - 1)
    def _(t):
        for lane in range(LANES):
            gather(lane, t).wait_send()

    @pl.loop(0, NZ)
    def _(block):
        for side in range(2):
            for width in range(2):

                @pl.when(jnp.logical_not((side * NZ + block == e) & (width == h)))
                def _():
                    for expert in range(2):
                        reply(expert, width, side, block).wait_send()


def shards(
    attn_input,
    query_grad,
    query_weight,
    moe_cotangent,
    expert_ids,
    route_weights,
    gate_saved,
    up_saved,
    gate_weight,
    up_weight,
    down_weight,
):
    vmem = pl.BlockSpec(memory_space=pltpu.VMEM)
    hbm = pl.BlockSpec(memory_space=pl.ANY)
    dma = pltpu.SemaphoreType.DMA
    tokens, width = moe_cotangent.shape
    slots, local, hidden = gate_saved.shape
    rows, model = query_weight.shape
    batch, heads = query_grad.shape
    units = hidden // 2
    q_wide, h_wide = model // LANES, local * units // LANES
    scratch = [
        pltpu.VMEM(query_grad.shape, BF),
        pltpu.VMEM((heads, batch), BF),
        pltpu.VMEM(attn_input.shape, BF),
        pltpu.VMEM(query_weight.shape, F32),
        pltpu.VMEM((2, slots, local, units), BF),
        pltpu.VMEM((2, slots, local, units), BF),
        pltpu.VMEM((2, local, width, units), BF),
        pltpu.VMEM((2, local, width, units), BF),
        pltpu.VMEM((2, local, units, width), BF),
        pltpu.VMEM((tokens, width), BF),
        pltpu.VMEM((local * NE, slots, tokens), BF),
        pltpu.VMEM((local * NE, slots, 1), F32),
        pltpu.VMEM((2, local * NE, slots, width), BF),
        pltpu.VMEM((2, local, NE, slots, width), BF),
        pltpu.VMEM((LANES, 2, NZ, rows, q_wide), BF),
        pltpu.VMEM((LANES, NZ - 1, 2, rows, q_wide), BF),
        pltpu.VMEM((LANES, rows, q_wide), BF),
        pltpu.VMEM((LANES, rows, q_wide), BF),
        pltpu.VMEM((LANES, 2, NZ, slots, h_wide), BF),
        pltpu.VMEM((LANES, NZ - 1, 2, slots, h_wide), BF),
        pltpu.VMEM((LANES, 2, NZ, slots, units), BF),
        pltpu.VMEM((local, 2, 2, NZ, slots, width), BF),
        pltpu.VMEM((2, NE, local, slots, width), BF),
        dma((8,)),
        dma((2, NE)),
        dma((2, NE)),
        dma((6,)),
        dma((6,)),
        dma((LANES, NZ - 1)),
        dma((LANES, NZ - 1)),
        dma((LANES,)),
        dma((LANES,)),
        dma((LANES, NZ - 1)),
        dma((LANES, NZ - 1)),
        dma((LANES, NZ - 1)),
        dma((LANES, NZ - 1)),
        dma((local, 2, 2, NZ)),
        dma((2, NE, local)),
    ]
    return pl.pallas_call(
        step_kernel,
        name="backward_step",
        out_shape=(
            jax.ShapeDtypeStruct((rows, model), F32),
            jax.ShapeDtypeStruct((tokens, width), F32),
        ),
        in_specs=[vmem, vmem, vmem] + [hbm] * 8,
        out_specs=(vmem, vmem),
        scratch_shapes=scratch,
        compiler_params=pltpu.CompilerParams(
            collective_id=0, has_side_effects=True, vmem_limit_bytes=58 << 20
        ),
    )(
        expert_ids.T,
        route_weights.T,
        moe_cotangent,
        query_grad,
        attn_input,
        query_weight,
        gate_saved,
        up_saved,
        gate_weight,
        up_weight,
        down_weight.reshape(local, 2, units, width),
    )


def solution(mesh):
    placed = (
        P("dp", None),
        P("dp", "expert"),
        P(("expert", "dp"), None),
        P("expert", "dp"),
        P("expert", None),
        P("expert", None),
        P("dp", "expert", None),
        P("dp", "expert", None),
        P("expert", "dp", None),
        P("expert", "dp", None),
        P("expert", None, "dp"),
    )
    return jax.shard_map(
        shards,
        mesh=mesh,
        in_specs=placed,
        out_specs=(P(("expert", "dp"), None), P("expert", "dp")),
        check_vma=False,
    )
```

time: 192 us -> 148 us (0.77)
  Pallas kernels: 188 us -> 144 us
    pallas_call x1, Pallas kernels: 188 us -> 144 us  [shards(): pl.pallas_call(step_kernel, name='backward_step', out_shape=(jax.ShapeDty...]
where the time goes in v3:
time: 148 us
  Pallas kernels  144 us (97%)
  local copies, waits for them, and re-layouts  3.44 us (2%)
    pallas_call x1, Pallas kernels, shards(): pl.pallas_call(step_kernel, name='backward_step', out_shape=(jax.ShapeDty...  144 us
    unnamed x2, local copies, waits for them, and re-layouts  3.44 us

profile of v3, /device:TPU:1, one launch (start us, length us, event | category | flops | bytes accessed | tf_op | source)
XLA Modules:
  0.0 148.1 jit_solution(1534436147026312255)
XLA Ops:
  0.6 144.0 %backward_step.1 = (f32[32,4096]{1,0:T(8,128)}, f32[128,256]{1,0:T(8,128)}) custom-call(s32[8,128]{1,0:T(8,128)} %bitcast.4, f32[8,128]{1,0:T(8,128)} %bitcast.5, bf16[128,256]{1,0:T(8,128)(2,1)} %cot_ref.1, bf16[768,512]{1,0:T(8,128)(2,1)} %grad_hbm.1, bf16[768,4096]{1,0:T(8,128)(2,1)} %input_hbm.1, f32[32,4096]{1,0:T(8,128)} %weight_hbm.1, ...), custom_call_target="tpu_custom_call" | custom-call | tf_op jit(solution)/shard_map/backward_step/pallas_call | solution.py:506
  144.7 1.9 %copy.15 = f32[32,4096]{1,0:T(8,128)} copy(f32[32,4096]{1,0:T(8,128)} %get-tuple-element.4) | data formatting | bytes 1048576
  146.5 1.6 %copy.16 = f32[128,256]{1,0:T(8,128)} copy(f32[128,256]{1,0:T(8,128)} %get-tuple-element.5) | data formatting | bytes 262144

commit v4 on v3

--- a/solution.py
+++ b/solution.py
@@ -13,6 +13,7 @@
 NZ = 8
 NE = 16
 LANES = 4
+RING_ORDER = (0, 2, 1, 3)
 NT = (((1,), (1,)), ((), ()))
 BF = jnp.bfloat16
 F32 = jnp.float32
@@ -58,6 +59,7 @@
     down_w,
     cot_in,
     onehot,
+    picks_t,
     scale,
     outgoing,
     arrived,
@@ -107,12 +109,21 @@
 
     own = pl.ds(pl.multiple_of(h * units, 128), units)
     other = pl.ds(pl.multiple_of((1 - h) * units, 128), units)
+    q_wide = q_part.shape[-1]
+
+    def strip(lane):
+        at = pl.ds(lane * q_wide, q_wide)
+        return (input_hbm.at[:, at], input_v.at[:, at])
+
     loads = [
         pltpu.make_async_copy(src, dst, load_sem.at[i])
         for i, (src, dst) in enumerate(
             (
                 (grad_hbm, grad_v),
-                (input_hbm, input_v),
+                strip(0),
+                strip(2),
+                strip(1),
+                strip(3),
                 (down_w_hbm.at[:, h], down_w.at[h]),
                 (gate_hbm.at[:, :, own], gate_v.at[h]),
                 (up_hbm.at[:, :, own], up_v.at[h]),
@@ -180,19 +191,13 @@
             rows = rows * scale[first : first + group].reshape(group * slots, 1)
             outgoing[side, first : first + group] = rows.astype(BF).reshape(group, slots, -1)
 
-    fill(h, cot_ref[...])
-
-    pl.semaphore_wait(barrier, 2 * NE + 1)
-    shares[0].start()
-    shares[1].start()
-
     def dispatch(side, k):
         to = lax.rem(e + k, NE)
         return remote(
             outgoing.at[side, pl.ds(2 * to, 2)],
             arrived.at[side, :, e],
-            disp_send.at[side, k],
-            disp_recv.at[side, k],
+            disp_send.at[side],
+            disp_recv.at[side],
             (to, d),
         )
 
@@ -203,21 +208,16 @@
 
         arrived[side, :, e] = outgoing[side, pl.ds(2 * e, 2)]
 
-    dispatch_all(h)
-    shares[0].wait_recv()
-    fill(1 - h, cot_in[...])
-    dispatch_all(1 - h)
-
     def ring(part, recv, send, got, lane, t):
         src = part.at[lane, :, at_z(lane, 1)] if isinstance(t, int) else recv.at[lane, t - 1]
-        return remote(src, recv.at[lane, t], send.at[lane, t], got.at[lane, t], toward(lane))
+        return remote(src, recv.at[lane, t], send, got.at[lane, t], toward(lane))
 
     def await_step(recv, send, got, lane, t):
         at = recv.at[lane, t]
-        remote(at, at, send.at[lane, t], got.at[lane, t], toward(lane)).wait_recv()
+        remote(at, at, send, got.at[lane, t], toward(lane)).wait_recv()
 
     def forward(part, recv, send, got, t):
-        for lane in range(LANES):
+        for lane in RING_ORDER:
             await_step(recv, send, got, lane, t - 1)
             total = recv[lane, t - 1].astype(F32) + part[lane, :, at_z(lane, 1 + t)].astype(F32)
             recv[lane, t - 1] = total.astype(BF)
@@ -229,12 +229,7 @@
     def h_forward(t):
         forward(h_part, h_recv, h_send, h_got, t)
 
-    loads[0].wait()
-    loads[1].wait()
-    grad_t[...] = grad_v[...].T
-    q_wide = q_part.shape[-1]
-    for lane in range(LANES):
-
+    def q_product(lane):
         @pl.loop(0, q_wide // 256)
         def _(j):
             columns = pl.ds(pl.multiple_of(lane * q_wide + j * 256, 256), 256)
@@ -243,23 +238,45 @@
                 BF
             ).reshape(2, NZ, 32, 256)
 
+    loads[0].wait()
+    grad_t[...] = grad_v[...].T
+    for i in (1, 2):
+        loads[i].wait()
+    for lane in (0, 2):
+        q_product(lane)
+
+    pl.semaphore_wait(barrier, 2 * NE + 1)
+    shares[0].start()
+    for lane in (0, 2):
         ring(q_part, q_recv, q_send, q_got, lane, 0).start()
-
-    @pl.loop(1, 3)
+    fill(h, cot_ref[...])
+    dispatch_all(h)
+    shares[1].start()
+    shares[0].wait_recv()
+    fill(1 - h, cot_in[...])
+    dispatch_all(1 - h)
+    for i in (3, 4):
+        loads[i].wait()
+    for lane in (1, 3):
+        q_product(lane)
+        ring(q_part, q_recv, q_send, q_got, lane, 0).start()
+
+    @pl.loop(1, 5)
     def _(t):
         q_forward(t)
 
-    @pl.loop(1, NE)
-    def _(k):
-        for side in range(2):
-            dispatch(side, k).wait_recv()
-
-    loads[2].wait()
     shares[1].wait_recv()
     for copy in shares[2:]:
         copy.start()
+
+    others = pl.ds(0, NE - 1)
+    for side in range(2):
+        at = arrived.at[side, :, others]
+        remote(at, at, disp_send.at[side], disp_recv.at[side], twin).wait_recv()
+
+    loads[5].wait()
     h_wide = h_part.shape[-1]
-    for lane in range(LANES):
+    for lane in RING_ORDER:
         expert, half = lane // 2, lane % 2
         rows = slice(half * h_wide, (half + 1) * h_wide)
 
@@ -277,20 +294,23 @@
 
         ring(h_part, h_recv, h_send, h_got, lane, 0).start()
 
-    @pl.loop(0, 3)
+    @pl.loop(0, 2)
     def _(p):
         h_forward(2 * p + 1)
         h_forward(2 * p + 2)
-        q_forward(p + 3)
-
-    q_forward(jnp.int32(NZ - 2))
+        q_forward(p + 5)
+
+    @pl.loop(5, NZ - 1)
+    def _(t):
+        h_forward(t)
+
     last = NZ - 2
 
     def gather(lane, t):
         at = grads.at[lane, :, at_z(lane, t)]
-        return remote(at, at, g_send.at[lane, t], g_got.at[lane, t], toward(lane))
-
-    for i in (3, 4, 5, 6, 7):
+        return remote(at, at, g_send, g_got.at[lane, t], toward(lane))
+
+    for i in (6, 7, 8, 9, 10):
         loads[i].wait()
     for i in (2, 3):
         shares[i].wait_recv()
@@ -320,50 +340,72 @@
         q_give[lane] = theirs.astype(BF)
         exchange(lane).start()
 
+    def place(expert, width, side, block):
+        return ((expert * 2 + width) * 2 + side) * NZ + block
+
     def reply(expert, width, side, block):
-        at = result.at[expert, width, side, block]
         return remote(
-            at,
+            result.at[place(expert, width, side, block)],
             returned.at[h, e, expert],
-            r_send.at[expert, width, side, block],
-            r_got.at[h, e, expert],
+            r_send,
+            r_got,
             (side * NZ + block, width * NZ + z),
         )
 
-    def produce(expert, block):
-        gate = grads[2 * expert, :, block].reshape(2 * slots, -1)
-        up = grads[2 * expert + 1, :, block].reshape(2 * slots, -1)
+    def relay(t, lanes=RING_ORDER):
+        for lane in lanes:
+            gather(lane, t).wait_recv()
+            gather(lane, t + 1).start()
+
+    def produce(expert, *hops):
+        blocks = [at_z(2 * expert, hop) for hop in hops]
+
+        def rows_of(lane):
+            parts = [grads[lane, :, block].reshape(2 * slots, units) for block in blocks]
+            return jnp.concatenate(parts, axis=0)
+
+        gate, up = rows_of(2 * expert), rows_of(2 * expert + 1)
         for width in range(2):
             rows = lax.dot_general(gate, gate_w[width, expert], NT, preferred_element_type=F32)
             rows = rows + lax.dot_general(
                 up, up_w[width, expert], NT, preferred_element_type=F32
             )
-            rows = rows.astype(BF).reshape(2, slots, -1)
-            for side in range(2):
-                result[expert, width, side, block] = rows[side]
-                here = (side * NZ + block == e) & (width == h)
-
-                @pl.when(here)
-                def _():
-                    returned[h, e, expert] = rows[side]
-
-                @pl.when(jnp.logical_not(here))
-                def _():
-                    reply(expert, width, side, block).start()
-
+            rows = rows.astype(BF).reshape(len(blocks), 2, slots, -1)
+            for i, block in enumerate(blocks):
+                for side in range(2):
+                    at = place(expert, width, side, block)
+                    result[at] = rows[i, side]
+                    here = (side * NZ + block == e) & (width == h)
+
+                    @pl.when(here)
+                    def _():
+                        pltpu.make_async_copy(
+                            result.at[at], returned.at[h, e, expert], r_got
+                        ).start()
+
+                    @pl.when(jnp.logical_not(here))
+                    def _():
+                        reply(expert, width, side, block).start()
+
+    @pl.loop(0, 4)
+    def _(t):
+        relay(t)
+
+    picks_t[...] = onehot[...].reshape(experts * slots, tokens).T
     for i in (4, 5):
         shares[i].wait_recv()
+    produce(0, 0, 1)
+    relay(jnp.int32(4), (0, 2))
+    produce(1, 0, 1)
+    relay(jnp.int32(4), (1, 3))
+    produce(0, 2, 3)
+    relay(jnp.int32(5), (0, 2))
+    produce(1, 2, 3)
+    relay(jnp.int32(5), (1, 3))
     for expert in range(2):
-        produce(expert, z)
-
-    @pl.loop(0, NZ - 2)
-    def _(t):
-        for lane in range(LANES):
-            gather(lane, t).wait_recv()
-            gather(lane, t + 1).start()
-
-        for expert in range(2):
-            produce(expert, at_z(2 * expert, t + 1))
+        produce(expert, 4, 5)
+    for expert in range(2):
+        produce(expert, 6)
 
     for lane in range(LANES):
         exchange(lane).wait_recv()
@@ -378,67 +420,35 @@
     stepped = weight - STEP_RATE * (gradient - radial * weight)
     norm = jnp.sum(stepped * stepped, axis=1, keepdims=True) * count + EPSILON
     query_out[...] = stepped * lax.rsqrt(norm)
+    for copy in shares:
+        copy.wait_send()
+    for side in range(2):
+        at = outgoing.at[side, pl.ds(0, 2 * NE - 2)]
+        remote(at, at, disp_send.at[side], disp_recv.at[side], twin).wait_send()
+    for recv, send, got in ((q_recv, q_send, q_got), (h_recv, h_send, h_got)):
+        remote(recv, recv, send, got.at[0, 0], twin).wait_send()
+    for lane in range(LANES):
+        exchange(lane).wait_send()
 
     for expert in range(2):
         for lane in (2 * expert, 2 * expert + 1):
             gather(lane, NZ - 2).wait_recv()
-        produce(expert, at_z(2 * expert, NZ - 1))
-
-    @pl.loop(0, NE)
-    def _(source):
-        for half in range(2):
-
-            @pl.when(jnp.logical_not((source == e) & (half == h)))
-            def _():
-                for expert in range(2):
-                    at = returned.at[half, source, expert]
-                    remote(
-                        at, at, r_send.at[expert, 0, 0, 0], r_got.at[half, source, expert], twin
-                    ).wait_recv()
-
-    total = 0.0
-    for half in range(2):
-        total = total + lax.dot_general(
-            onehot[...].reshape(experts * slots, tokens),
+        produce(expert, NZ - 1)
+
+    remote(returned, returned, r_send, r_got, twin).wait_recv()
+    moe_out[...] = sum(
+        jnp.dot(
+            picks_t[...],
             returned[half].reshape(experts * slots, -1),
-            (((0,), (0,)), ((), ())),
             preferred_element_type=F32,
         )
-    moe_out[...] = total
-
-    for copy in shares:
-        copy.wait_send()
-
-    @pl.loop(1, NE)
-    def _(k):
-        for side in range(2):
-            dispatch(side, k).wait_send()
-
-    for lane in range(LANES):
-        ring(q_part, q_recv, q_send, q_got, lane, 0).wait_send()
-        ring(h_part, h_recv, h_send, h_got, lane, 0).wait_send()
-        exchange(lane).wait_send()
-
-    @pl.loop(1, NZ - 1)
-    def _(t):
-        for lane in range(LANES):
-            ring(q_part, q_recv, q_send, q_got, lane, t).wait_send()
-            ring(h_part, h_recv, h_send, h_got, lane, t).wait_send()
-
-    @pl.loop(0, NZ - 1)
-    def _(t):
-        for lane in range(LANES):
-            gather(lane, t).wait_send()
-
-    @pl.loop(0, NZ)
-    def _(block):
-        for side in range(2):
-            for width in range(2):
-
-                @pl.when(jnp.logical_not((side * NZ + block == e) & (width == h)))
-                def _():
-                    for expert in range(2):
-                        reply(expert, width, side, block).wait_send()
+        for half in range(2)
+    )
+
+    at = grads.at[:, :, pl.ds(0, NZ - 1)]
+    remote(at, at, g_send, g_got.at[0, 0], twin).wait_send()
+    at = result.at[pl.ds(0, result.shape[0] - 2)]
+    remote(at, at, r_send, r_got, twin).wait_send()
 
 
 def shards(
@@ -475,6 +485,7 @@
         pltpu.VMEM((2, local, units, width), BF),
         pltpu.VMEM((tokens, width), BF),
         pltpu.VMEM((local * NE, slots, tokens), BF),
+        pltpu.VMEM((tokens, local * NE * slots), BF),
         pltpu.VMEM((local * NE, slots, 1), F32),
         pltpu.VMEM((2, local * NE, slots, width), BF),
         pltpu.VMEM((2, local, NE, slots, width), BF),
@@ -485,23 +496,23 @@
         pltpu.VMEM((LANES, 2, NZ, slots, h_wide), BF),
         pltpu.VMEM((LANES, NZ - 1, 2, slots, h_wide), BF),
         pltpu.VMEM((LANES, 2, NZ, slots, units), BF),
-        pltpu.VMEM((local, 2, 2, NZ, slots, width), BF),
+        pltpu.VMEM((local * 4 * NZ, slots, width), BF),
         pltpu.VMEM((2, NE, local, slots, width), BF),
-        dma((8,)),
-        dma((2, NE)),
-        dma((2, NE)),
+        dma((11,)),
+        dma((2,)),
+        dma((2,)),
         dma((6,)),
         dma((6,)),
-        dma((LANES, NZ - 1)),
+        dma,
         dma((LANES, NZ - 1)),
         dma((LANES,)),
         dma((LANES,)),
+        dma,
         dma((LANES, NZ - 1)),
+        dma,
         dma((LANES, NZ - 1)),
-        dma((LANES, NZ - 1)),
-        dma((LANES, NZ - 1)),
-        dma((local, 2, 2, NZ)),
-        dma((2, NE, local)),
+        dma,
+        dma,
     ]
     return pl.pallas_call(
         step_kernel,

time: 148 us -> 137 us (0.926)
  Pallas kernels: 144 us -> 133 us
    pallas_call x1, Pallas kernels: 144 us -> 133 us  [shards(): pl.pallas_call(step_kernel, name='backward_step', out_shape=(jax.ShapeDty...]
where the time goes in v4:
time: 137 us
  Pallas kernels  133 us (97%)
  local copies, waits for them, and re-layouts  3.44 us (3%)
    pallas_call x1, Pallas kernels, shards(): pl.pallas_call(step_kernel, name='backward_step', out_shape=(jax.ShapeDty...  133 us
    unnamed x2, local copies, waits for them, and re-layouts  3.44 us

profile of v4, /device:TPU:1, one launch (start us, length us, event | category | flops | bytes accessed | tf_op | source)
XLA Modules:
  0.0 137.2 jit_solution(16321752356815402070)
XLA Ops:
  0.6 133.1 %backward_step.1 = (f32[32,4096]{1,0:T(8,128)}, f32[128,256]{1,0:T(8,128)}) custom-call(s32[8,128]{1,0:T(8,128)} %bitcast.4, f32[8,128]{1,0:T(8,128)} %bitcast.5, bf16[128,256]{1,0:T(8,128)(2,1)} %cot_ref.1, bf16[768,512]{1,0:T(8,128)(2,1)} %grad_hbm.1, bf16[768,4096]{1,0:T(8,128)(2,1)} %input_hbm.1, f32[32,4096]{1,0:T(8,128)} %weight_hbm.1, ...), custom_call_target="tpu_custom_call" | custom-call | tf_op jit(solution)/shard_map/backward_step/pallas_call | solution.py:517
  133.7 1.9 %copy.15 = f32[32,4096]{1,0:T(8,128)} copy(f32[32,4096]{1,0:T(8,128)} %get-tuple-element.4) | data formatting | bytes 1048576
  135.6 1.6 %copy.16 = f32[128,256]{1,0:T(8,128)} copy(f32[128,256]{1,0:T(8,128)} %get-tuple-element.5) | data formatting | bytes 262144

commit v5 on v4

--- a/solution.py
+++ b/solution.py
@@ -13,7 +13,9 @@
 NZ = 8
 NE = 16
 LANES = 4
-RING_ORDER = (0, 2, 1, 3)
+LONG = ((0, 1, 4), (2, -1, 4), (1, 1, 4), (3, -1, 4))
+SHORT = ((0, -1, 3), (2, 1, 3), (1, -1, 3), (3, 1, 3))
+CHAINS = LONG + SHORT
 NT = (((1,), (1,)), ((), ()))
 BF = jnp.bfloat16
 F32 = jnp.float32
@@ -30,8 +32,8 @@
     )
 
 
-def sign(lane):
-    return 1 if lane < 2 else -1
+def slot(way, t):
+    return t if way > 0 else NZ // 2 + t
 
 
 def step_kernel(
@@ -101,11 +103,11 @@
     experts = 2 * NE
     tokens = ids_ref.shape[1]
 
-    def toward(lane):
-        return ahead if sign(lane) > 0 else behind
-
-    def at_z(lane, hops):
-        return lax.rem(z + 4 * NZ - sign(lane) * hops, NZ)
+    def toward(way):
+        return ahead if way > 0 else behind
+
+    def at_z(offset):
+        return lax.rem(z + 2 * NZ + offset, NZ)
 
     own = pl.ds(pl.multiple_of(h * units, 128), units)
     other = pl.ds(pl.multiple_of((1 - h) * units, 128), units)
@@ -208,20 +210,41 @@
 
         arrived[side, :, e] = outgoing[side, pl.ds(2 * e, 2)]
 
-    def ring(part, recv, send, got, lane, t):
-        src = part.at[lane, :, at_z(lane, 1)] if isinstance(t, int) else recv.at[lane, t - 1]
-        return remote(src, recv.at[lane, t], send, got.at[lane, t], toward(lane))
-
-    def await_step(recv, send, got, lane, t):
-        at = recv.at[lane, t]
-        remote(at, at, send, got.at[lane, t], toward(lane)).wait_recv()
+    def ring(part, recv, send, got, chain, t):
+        lane, way, hops = chain
+        src = part.at[lane, :, at_z(way * hops)] if t == 0 else recv.at[lane, slot(way, t - 1)]
+        at = slot(way, t)
+        return remote(src, recv.at[lane, at], send, got.at[lane, at], toward(way))
+
+    def await_step(recv, send, got, chain, t):
+        lane, way, _ = chain
+        at = recv.at[lane, slot(way, t)]
+        remote(at, at, send, got.at[lane, slot(way, t)], toward(way)).wait_recv()
+
+    def begin(part, recv, send, got, lane):
+        for chain in CHAINS:
+            if chain[0] == lane:
+                ring(part, recv, send, got, chain, 0).start()
 
     def forward(part, recv, send, got, t):
-        for lane in RING_ORDER:
-            await_step(recv, send, got, lane, t - 1)
-            total = recv[lane, t - 1].astype(F32) + part[lane, :, at_z(lane, 1 + t)].astype(F32)
-            recv[lane, t - 1] = total.astype(BF)
-            ring(part, recv, send, got, lane, t).start()
+        for chain in CHAINS if t < 3 else LONG:
+            lane, way, hops = chain
+            await_step(recv, send, got, chain, t - 1)
+            at = slot(way, t - 1)
+            own_part = part[lane, :, at_z(way * (hops - t))]
+            recv[lane, at] = (recv[lane, at].astype(F32) + own_part.astype(F32)).astype(BF)
+            ring(part, recv, send, got, chain, t).start()
+
+    def finish(recv, send, got, lane):
+        for chain in CHAINS:
+            if chain[0] == lane:
+                await_step(recv, send, got, chain, chain[2] - 1)
+
+    def summed(part, recv, lane, side):
+        long = 1 if lane < 2 else -1
+        both = recv[lane, slot(long, 3), side].astype(F32)
+        both = both + recv[lane, slot(-long, 2), side].astype(F32)
+        return both + part[lane, side, z].astype(F32)
 
     def q_forward(t):
         forward(q_part, q_recv, q_send, q_got, t)
@@ -248,7 +271,7 @@
     pl.semaphore_wait(barrier, 2 * NE + 1)
     shares[0].start()
     for lane in (0, 2):
-        ring(q_part, q_recv, q_send, q_got, lane, 0).start()
+        begin(q_part, q_recv, q_send, q_got, lane)
     fill(h, cot_ref[...])
     dispatch_all(h)
     shares[1].start()
@@ -259,12 +282,10 @@
         loads[i].wait()
     for lane in (1, 3):
         q_product(lane)
-        ring(q_part, q_recv, q_send, q_got, lane, 0).start()
-
-    @pl.loop(1, 5)
-    def _(t):
-        q_forward(t)
-
+        begin(q_part, q_recv, q_send, q_got, lane)
+
+    q_forward(1)
+    q_forward(2)
     shares[1].wait_recv()
     for copy in shares[2:]:
         copy.start()
@@ -276,7 +297,7 @@
 
     loads[5].wait()
     h_wide = h_part.shape[-1]
-    for lane in RING_ORDER:
+    for lane in range(LANES):
         expert, half = lane // 2, lane % 2
         rows = slice(half * h_wide, (half + 1) * h_wide)
 
@@ -292,23 +313,17 @@
                 )
             h_part[lane, block_side] = part.astype(BF).reshape(NZ, slots, h_wide)
 
-        ring(h_part, h_recv, h_send, h_got, lane, 0).start()
-
-    @pl.loop(0, 2)
-    def _(p):
-        h_forward(2 * p + 1)
-        h_forward(2 * p + 2)
-        q_forward(p + 5)
-
-    @pl.loop(5, NZ - 1)
-    def _(t):
-        h_forward(t)
-
-    last = NZ - 2
-
-    def gather(lane, t):
-        at = grads.at[lane, :, at_z(lane, t)]
-        return remote(at, at, g_send, g_got.at[lane, t], toward(lane))
+        begin(h_part, h_recv, h_send, h_got, lane)
+
+    h_forward(1)
+    q_forward(3)
+    h_forward(2)
+    h_forward(3)
+
+    def gather(chain, t):
+        lane, way, _ = chain
+        at = grads.at[lane, :, at_z(-way * t)]
+        return remote(at, at, g_send, g_got.at[lane, slot(way, t)], toward(way))
 
     for i in (6, 7, 8, 9, 10):
         loads[i].wait()
@@ -317,10 +332,10 @@
     for expert in range(2):
         for half in range(2):
             lane = 2 * expert + half
-            await_step(h_recv, h_send, h_got, lane, last)
+            finish(h_recv, h_send, h_got, lane)
             columns = slice(half * h_wide, (half + 1) * h_wide)
             for side in range(2):
-                hidden = h_recv[lane, last, side].astype(F32) + h_part[lane, side, z].astype(F32)
+                hidden = summed(h_part, h_recv, lane, side)
                 g = gate_v[side, :, expert, columns].astype(F32)
                 u = up_v[side, :, expert, columns].astype(F32)
                 sigma = 1.0 / (1.0 + jnp.exp(-g))
@@ -328,16 +343,16 @@
                     hidden * u * sigma * (1.0 + g * (1.0 - sigma))
                 ).astype(BF)
                 grads[2 * expert + 1, side, z, :, columns] = (hidden * g * sigma).astype(BF)
-        for lane in (2 * expert, 2 * expert + 1):
-            gather(lane, 0).start()
+        for chain in CHAINS:
+            if chain[0] // 2 == expert:
+                gather(chain, 0).start()
 
     def exchange(lane):
         return remote(q_give.at[lane], q_take.at[lane], qx_send.at[lane], qx_got.at[lane], twin)
 
     for lane in range(LANES):
-        await_step(q_recv, q_send, q_got, lane, last)
-        theirs = q_recv[lane, last, 1 - h].astype(F32) + q_part[lane, 1 - h, z].astype(F32)
-        q_give[lane] = theirs.astype(BF)
+        finish(q_recv, q_send, q_got, lane)
+        q_give[lane] = summed(q_part, q_recv, lane, 1 - h).astype(BF)
         exchange(lane).start()
 
     def place(expert, width, side, block):
@@ -352,13 +367,14 @@
             (side * NZ + block, width * NZ + z),
         )
 
-    def relay(t, lanes=RING_ORDER):
-        for lane in lanes:
-            gather(lane, t).wait_recv()
-            gather(lane, t + 1).start()
-
-    def produce(expert, *hops):
-        blocks = [at_z(2 * expert, hop) for hop in hops]
+    def relay(t, chains=CHAINS):
+        for chain in chains:
+            gather(chain, t).wait_recv()
+            if t + 1 < chain[2]:
+                gather(chain, t + 1).start()
+
+    def produce(expert, *offsets):
+        blocks = [at_z(offset) for offset in offsets]
 
         def rows_of(lane):
             parts = [grads[lane, :, block].reshape(2 * slots, units) for block in blocks]
@@ -387,29 +403,13 @@
                     def _():
                         reply(expert, width, side, block).start()
 
-    @pl.loop(0, 4)
-    def _(t):
-        relay(t)
-
+    relay(0)
     picks_t[...] = onehot[...].reshape(experts * slots, tokens).T
-    for i in (4, 5):
-        shares[i].wait_recv()
-    produce(0, 0, 1)
-    relay(jnp.int32(4), (0, 2))
-    produce(1, 0, 1)
-    relay(jnp.int32(4), (1, 3))
-    produce(0, 2, 3)
-    relay(jnp.int32(5), (0, 2))
-    produce(1, 2, 3)
-    relay(jnp.int32(5), (1, 3))
-    for expert in range(2):
-        produce(expert, 4, 5)
-    for expert in range(2):
-        produce(expert, 6)
+    relay(1)
 
     for lane in range(LANES):
         exchange(lane).wait_recv()
-        mine = q_recv[lane, last, h].astype(F32) + q_part[lane, h, z].astype(F32)
+        mine = summed(q_part, q_recv, lane, h)
         query_out[:, lane * q_wide : (lane + 1) * q_wide] = mine + q_take[lane].astype(F32)
     gradient = query_out[...]
     weight = weight_v[...]
@@ -420,20 +420,31 @@
     stepped = weight - STEP_RATE * (gradient - radial * weight)
     norm = jnp.sum(stepped * stepped, axis=1, keepdims=True) * count + EPSILON
     query_out[...] = stepped * lax.rsqrt(norm)
+
+    for i in (4, 5):
+        shares[i].wait_recv()
+    produce(0, 0, 1, -1)
+    produce(1, 0, 1, -1)
+    relay(2, LONG)
+    produce(0, 2, -2)
+    produce(1, 2, -2)
+    relay(2, SHORT)
+    produce(0, 3, -3)
+    produce(1, 3, -3)
     for copy in shares:
         copy.wait_send()
     for side in range(2):
         at = outgoing.at[side, pl.ds(0, 2 * NE - 2)]
         remote(at, at, disp_send.at[side], disp_recv.at[side], twin).wait_send()
     for recv, send, got in ((q_recv, q_send, q_got), (h_recv, h_send, h_got)):
-        remote(recv, recv, send, got.at[0, 0], twin).wait_send()
+        at = recv.at[:, pl.ds(0, NZ - 1)]
+        remote(at, at, send, got.at[0, 0], twin).wait_send()
     for lane in range(LANES):
         exchange(lane).wait_send()
 
     for expert in range(2):
-        for lane in (2 * expert, 2 * expert + 1):
-            gather(lane, NZ - 2).wait_recv()
-        produce(expert, NZ - 1)
+        relay(3, [chain for chain in LONG if chain[0] // 2 == expert])
+        produce(expert, 4)
 
     remote(returned, returned, r_send, r_got, twin).wait_recv()
     moe_out[...] = sum(
@@ -490,11 +501,11 @@
         pltpu.VMEM((2, local * NE, slots, width), BF),
         pltpu.VMEM((2, local, NE, slots, width), BF),
         pltpu.VMEM((LANES, 2, NZ, rows, q_wide), BF),
-        pltpu.VMEM((LANES, NZ - 1, 2, rows, q_wide), BF),
+        pltpu.VMEM((LANES, NZ, 2, rows, q_wide), BF),
         pltpu.VMEM((LANES, rows, q_wide), BF),
         pltpu.VMEM((LANES, rows, q_wide), BF),
         pltpu.VMEM((LANES, 2, NZ, slots, h_wide), BF),
-        pltpu.VMEM((LANES, NZ - 1, 2, slots, h_wide), BF),
+        pltpu.VMEM((LANES, NZ, 2, slots, h_wide), BF),
         pltpu.VMEM((LANES, 2, NZ, slots, units), BF),
         pltpu.VMEM((local * 4 * NZ, slots, width), BF),
         pltpu.VMEM((2, NE, local, slots, width), BF),
@@ -504,13 +515,13 @@
         dma((6,)),
         dma((6,)),
         dma,
-        dma((LANES, NZ - 1)),
+        dma((LANES, NZ)),
         dma((LANES,)),
         dma((LANES,)),
         dma,
-        dma((LANES, NZ - 1)),
+        dma((LANES, NZ)),
         dma,
-        dma((LANES, NZ - 1)),
+        dma((LANES, NZ)),
         dma,
         dma,
     ]

time: 137 us -> 131 us (0.956)
  the two profiles are of different devices: /device:TPU:1 before, /device:TPU:4 now
where the time goes in v5:
time: 131 us
  Pallas kernels  127 us (97%)
  local copies, waits for them, and re-layouts  3.44 us (3%)
    pallas_call x1, Pallas kernels, shards(): pl.pallas_call(step_kernel, name='backward_step', out_shape=(jax.ShapeDty...  127 us
    unnamed x2, local copies, waits for them, and re-layouts  3.44 us

profile of v5, /device:TPU:4, one launch (start us, length us, event | category | flops | bytes accessed | tf_op | source)
XLA Modules:
  0.0 131.2 jit_solution(823284755124680730)
XLA Ops:
  0.6 127.2 %backward_step.1 = (f32[32,4096]{1,0:T(8,128)}, f32[128,256]{1,0:T(8,128)}) custom-call(s32[8,128]{1,0:T(8,128)} %bitcast.4, f32[8,128]{1,0:T(8,128)} %bitcast.5, bf16[128,256]{1,0:T(8,128)(2,1)} %cot_ref.1, bf16[768,512]{1,0:T(8,128)(2,1)} %grad_hbm.1, bf16[768,4096]{1,0:T(8,128)(2,1)} %input_hbm.1, f32[32,4096]{1,0:T(8,128)} %weight_hbm.1, ...), custom_call_target="tpu_custom_call" | custom-call | tf_op jit(solution)/shard_map/backward_step/pallas_call | solution.py:528
  127.8 1.9 %copy.15 = f32[32,4096]{1,0:T(8,128)} copy(f32[32,4096]{1,0:T(8,128)} %get-tuple-element.4) | data formatting | bytes 1048576
  129.7 1.6 %copy.16 = f32[128,256]{1,0:T(8,128)} copy(f32[128,256]{1,0:T(8,128)} %get-tuple-element.5) | data formatting | bytes 262144

commit v6 on v5

--- a/solution.py
+++ b/solution.py
@@ -263,18 +263,18 @@
 
     loads[0].wait()
     grad_t[...] = grad_v[...].T
-    for i in (1, 2):
-        loads[i].wait()
-    for lane in (0, 2):
-        q_product(lane)
+    loads[1].wait()
+    q_product(0)
 
     pl.semaphore_wait(barrier, 2 * NE + 1)
     shares[0].start()
-    for lane in (0, 2):
-        begin(q_part, q_recv, q_send, q_got, lane)
+    begin(q_part, q_recv, q_send, q_got, 0)
     fill(h, cot_ref[...])
     dispatch_all(h)
     shares[1].start()
+    loads[2].wait()
+    q_product(2)
+    begin(q_part, q_recv, q_send, q_got, 2)
     shares[0].wait_recv()
     fill(1 - h, cot_in[...])
     dispatch_all(1 - h)
@@ -460,6 +460,11 @@
     remote(at, at, g_send, g_got.at[0, 0], twin).wait_send()
     at = result.at[pl.ds(0, result.shape[0] - 2)]
     remote(at, at, r_send, r_got, twin).wait_send()
+
+
+def store_kernel(query_in, moe_in, query_out, moe_out):
+    query_out[...] = query_in[...]
+    moe_out[...] = moe_in[...]
 
 
 def shards(
@@ -525,7 +530,7 @@
         dma,
         dma,
     ]
-    return pl.pallas_call(
+    results = pl.pallas_call(
         step_kernel,
         name="backward_step",
         out_shape=(
@@ -551,6 +556,13 @@
         up_weight,
         down_weight.reshape(local, 2, units, width),
     )
+    return pl.pallas_call(
+        store_kernel,
+        name="store_results",
+        out_shape=tuple(jax.ShapeDtypeStruct(r.shape, r.dtype) for r in results),
+        in_specs=[vmem] * 2,
+        out_specs=(vmem, vmem),
+    )(*results)
 
 
 def solution(mesh):

time: 131 us -> 128 us (0.977)
  local copies, waits for them, and re-layouts: 3.44 us -> 0 us
    unnamed x2 -> x0, local copies, waits for them, and re-layouts: 3.44 us -> none
    pallas_call x1, Pallas kernels: 127 us -> 125 us  [shards(): pl.pallas_call(step_kernel, name='backward_step', out_shape=(jax.ShapeDty...]
    pallas_call x0 -> x1, Pallas kernels: none -> 1.93 us  [shards(): pl.pallas_call(store_kernel, name='store_results', out_shape=tuple((jax.S...]
where the time goes in v6:
time: 128 us
  Pallas kernels  127 us (99%)
    pallas_call x1, Pallas kernels, shards(): pl.pallas_call(step_kernel, name='backward_step', out_shape=(jax.ShapeDty...  125 us

profile of v6, /device:TPU:4, one launch (start us, length us, event | category | flops | bytes accessed | tf_op | source)
XLA Modules:
  0.0 127.6 jit_solution(14080609937265569889)
XLA Ops:
  0.6 125.1 %backward_step.1 = (f32[32,4096]{1,0:T(8,128)}, f32[128,256]{1,0:T(8,128)}) custom-call(s32[8,128]{1,0:T(8,128)} %bitcast.4, f32[8,128]{1,0:T(8,128)} %bitcast.5, bf16[128,256]{1,0:T(8,128)(2,1)} %cot_ref.1, bf16[768,512]{1,0:T(8,128)(2,1)} %grad_hbm.1, bf16[768,4096]{1,0:T(8,128)(2,1)} %input_hbm.1, f32[32,4096]{1,0:T(8,128)} %weight_hbm.1, ...), custom_call_target="tpu_custom_call" | custom-call | tf_op jit(solution)/shard_map/backward_step/pallas_call | solution.py:533
  125.7 1.9 %store_results.1 = (f32[32,4096]{1,0:T(8,128)}, f32[128,256]{1,0:T(8,128)}) custom-call(f32[32,4096]{1,0:T(8,128)} %get-tuple-element.4.query_in, f32[128,256]{1,0:T(8,128)} %get-tuple-element.5.moe_in), custom_call_target="tpu_custom_call" | custom-call | tf_op jit(solution)/shard_map/store_results/pallas_call | solution.py:559

commit v7 on v6

--- a/solution.py
+++ b/solution.py
@@ -424,8 +424,8 @@
     for i in (4, 5):
         shares[i].wait_recv()
     produce(0, 0, 1, -1)
+    relay(2, LONG)
     produce(1, 0, 1, -1)
-    relay(2, LONG)
     produce(0, 2, -2)
     produce(1, 2, -2)
     relay(2, SHORT)

time: 128 us -> 128 us (level)
  no operation moved by 1% of the time
where the time goes in v7:
time: 128 us
  Pallas kernels  127 us (99%)
    pallas_call x1, Pallas kernels, shards(): pl.pallas_call(step_kernel, name='backward_step', out_shape=(jax.ShapeDty...  125 us

profile of v7, /device:TPU:4, one launch (start us, length us, event | category | flops | bytes accessed | tf_op | source)
XLA Modules:
  0.0 128.0 jit_solution(17199697799852720466)
XLA Ops:
  0.6 125.4 %backward_step.1 = (f32[32,4096]{1,0:T(8,128)}, f32[128,256]{1,0:T(8,128)}) custom-call(s32[8,128]{1,0:T(8,128)} %bitcast.4, f32[8,128]{1,0:T(8,128)} %bitcast.5, bf16[128,256]{1,0:T(8,128)(2,1)} %cot_ref.1, bf16[768,512]{1,0:T(8,128)(2,1)} %grad_hbm.1, bf16[768,4096]{1,0:T(8,128)(2,1)} %input_hbm.1, f32[32,4096]{1,0:T(8,128)} %weight_hbm.1, ...), custom_call_target="tpu_custom_call" | custom-call | tf_op jit(solution)/shard_map/backward_step/pallas_call | solution.py:533
  126.1 1.9 %store_results.1 = (f32[32,4096]{1,0:T(8,128)}, f32[128,256]{1,0:T(8,128)}) custom-call(f32[32,4096]{1,0:T(8,128)} %get-tuple-element.4.query_in, f32[128,256]{1,0:T(8,128)} %get-tuple-element.5.moe_in), custom_call_target="tpu_custom_call" | custom-call | tf_op jit(solution)/shard_map/store_results/pallas_call | solution.py:559
